TPU v7x, 512 devices: a whole 4x4x16 slice. The times are simulated.
512 devices in a mesh: ctx: 64 (over z, y), tp: 8 (over x, core).
Axes of the slice: x: 4, y: 4, z: 16, core: 2. Of those that a mesh axis runs over, the one named last changes fastest.
Arguments:
- queries: bfloat16 [8192, 4096], P('ctx', 'tp'), may hold values from -6 to 6
- keys: bfloat16 [8192, 1024], P('ctx', 'tp'), may hold values from -6 to 6
- values: bfloat16 [8192, 1024], P('ctx', 'tp'), may hold values from -4 to 4
- w_out: bfloat16 [4096, 4096], P('tp'), may hold values from -0.09375 to 0.09375
- relevance_out: bfloat16 [8192, 4096], P('ctx', 'tp'), may hold values from -4 to 4
- segment_ids: int32 [8192], replicated, may hold values from 0 to 31, never falling along the last dimension, each value on 1 to 1024 neighbouring positions
Outputs:
- relevance_heads: bfloat16 [8192, 4096], P('ctx', 'tp')
- relevance_tokens: float32 [8192, 8], P('ctx', 'tp')
Inputs may be any that keep to these rules, and one draw needn't show every extreme that they name: `segment_ids`: ids never fall along the prompt; every document holds 1 to 1024 tokens and one holds exactly 1024.
All inputs are finite; a program needn't handle non-finite values.
Results may differ from a plain program's by a relative error of at most 0.02.
Values may be sent and summed in bfloat16 or wider, within the bound.
A program may use at most 64 MiB of HBM per device.

v0:
```python
import jax
import jax.numpy as jnp
from jax import lax
from jax.sharding import PartitionSpec as P

HEAD_DIM = 128
REACH = 8
KBLK = 512
GROUP = 4


masked_score = -1e30


def passed_along(shard, axis, by):
    count = lax.axis_size(axis)
    pairs = [(i, i + by) for i in range(count) if 0 <= i + by < count]
    return lax.ppermute(shard, axis, pairs)


def masked_scores(query_rows, key_block, row_segment, row_position, key_segment, key_position):
    scores = jnp.einsum(
        "krd,jkd->krj", query_rows, key_block, preferred_element_type=jnp.float32
    ) * HEAD_DIM ** (-0.5)
    visible = (row_segment[:, None] == key_segment[None, :]) & (
        key_position[None, :] <= row_position[:, None]
    )
    return (scores, visible[None])


def to_rows(matrix, tokens, local_groups):
    return (
        matrix.reshape(tokens, local_groups, GROUP, HEAD_DIM)
        .transpose(1, 0, 2, 3)
        .reshape(local_groups, tokens * GROUP, HEAD_DIM)
    )


def on_device(queries, keys, values, w_out, relevance_out, segment_ids):
    tokens = queries.shape[0]
    local_groups = keys.shape[1] // HEAD_DIM
    row_count = tokens * GROUP
    shard_index = lax.axis_index("ctx")
    first_token = shard_index * tokens
    query_rows = to_rows(queries, tokens, local_groups)
    own_segment = lax.dynamic_slice_in_dim(segment_ids, first_token, tokens)
    row_segment = jnp.repeat(own_segment, GROUP)
    row_position = first_token + jnp.repeat(jnp.arange(tokens, dtype=jnp.int32), GROUP)
    earlier = []
    for distance in range(REACH, 0, -1):
        earlier.append(passed_along((keys, values), "ctx", distance))
    window_length = ((REACH + 1) * tokens + KBLK - 1) // KBLK * KBLK
    pad_rows = window_length - (REACH + 1) * tokens
    filler = jnp.zeros((pad_rows, keys.shape[1]), keys.dtype)
    key_window = jnp.concatenate([piece[0] for piece in earlier] + [keys, filler], axis=0)
    value_window = jnp.concatenate([piece[1] for piece in earlier] + [values, filler], axis=0)
    offset = first_token - REACH * tokens
    padded_segments = jnp.concatenate(
        [
            jnp.full((window_length,), -1, jnp.int32),
            segment_ids,
            jnp.full((window_length,), -1, jnp.int32),
        ]
    )
    key_segment = lax.dynamic_slice_in_dim(padded_segments, offset + window_length, window_length)
    key_heads = key_window.reshape(window_length, local_groups, HEAD_DIM)
    value_heads = value_window.reshape(window_length, local_groups, HEAD_DIM)
    doc_start = jnp.sum((segment_ids < own_segment[0]).astype(jnp.int32))
    low_block = (doc_start - offset) // KBLK
    high_block = (first_token + tokens - 1 - offset) // KBLK + 1

    def block_inputs(block):
        start = block * KBLK
        key_block = lax.dynamic_slice_in_dim(key_heads, start, KBLK, 0)
        value_block = lax.dynamic_slice_in_dim(value_heads, start, KBLK, 0)
        segment_block = lax.dynamic_slice_in_dim(key_segment, start, KBLK)
        position_block = offset + start + jnp.arange(KBLK, dtype=jnp.int32)
        scores, visible = masked_scores(
            query_rows, key_block, row_segment, row_position, segment_block, position_block
        )
        return (start, value_block, scores, visible)

    def forward_block(block, carry):
        row_max, total, summed = carry
        start, value_block, scores, visible = block_inputs(block)
        new_max = jnp.maximum(row_max, jnp.max(jnp.where(visible, scores, masked_score), axis=2))
        weights = jnp.where(visible, jnp.exp(scores - new_max[..., None]), 0.0)
        rescale = jnp.exp(row_max - new_max)
        total = total * rescale + jnp.sum(weights, axis=2)
        summed = summed * rescale[..., None] + jnp.einsum(
            "krj,jkd->krd",
            weights.astype(jnp.bfloat16),
            value_block,
            preferred_element_type=jnp.float32,
        )
        return (new_max, total, summed)

    start_carry = (
        jnp.full((local_groups, row_count), masked_score, jnp.float32),
        jnp.zeros((local_groups, row_count), jnp.float32),
        jnp.zeros((local_groups, row_count, HEAD_DIM), jnp.float32),
    )
    row_max, total, summed = lax.fori_loop(low_block, high_block, forward_block, start_carry)
    attention_rows = (summed / total[..., None]).astype(jnp.bfloat16)
    attention = (
        attention_rows.reshape(local_groups, tokens, GROUP, HEAD_DIM)
        .transpose(1, 0, 2, 3)
        .reshape(tokens, local_groups * GROUP * HEAD_DIM)
    )
    totals = lax.psum(jnp.dot(attention, w_out, preferred_element_type=jnp.float32), "tp")
    upper = lax.all_gather(relevance_out, "tp", axis=1, tiled=True).astype(jnp.float32)
    ratio = (upper * totals / (totals * totals + 1.0)).astype(jnp.bfloat16)
    carried_back = lax.dot_general(
        ratio, w_out, (((1,), (1,)), ((), ())), preferred_element_type=jnp.float32
    )
    attention_float = attention.astype(jnp.float32)
    carried = attention_float * carried_back
    relevance_heads = carried.astype(jnp.bfloat16)
    passed = (carried * attention_float / (attention_float * attention_float + 1.0)).astype(
        jnp.bfloat16
    )
    passed_rows = to_rows(passed, tokens, local_groups)

    def backward_block(block, terms):
        start, value_block, scores, visible = block_inputs(block)
        share = jnp.where(visible, jnp.exp(scores - row_max[..., None]), 0.0) / total[..., None]
        inner = jnp.einsum(
            "krd,jkd->krj", passed_rows, value_block, preferred_element_type=jnp.float32
        )
        added = jnp.sum(share * inner, axis=1)
        current = lax.dynamic_slice_in_dim(terms, start, KBLK, 1)
        return lax.dynamic_update_slice_in_dim(terms, current + added, start, 1)

    terms = lax.fori_loop(
        low_block, high_block, backward_block, jnp.zeros((local_groups, window_length), jnp.float32)
    )
    own_terms = lax.dynamic_slice_in_dim(terms, first_token - offset, tokens, 1)
    for distance in range(1, REACH + 1):
        piece = lax.dynamic_slice_in_dim(terms, first_token - distance * tokens - offset, tokens, 1)
        own_terms = own_terms + passed_along(piece, "ctx", -distance)
    return (relevance_heads, own_terms.T)


def solution(mesh):
    placed = (P("ctx", "tp"), P("ctx", "tp"), P("ctx", "tp"), P("tp", None), P("ctx", "tp"), P())
    return jax.shard_map(
        on_device,
        mesh=mesh,
        in_specs=placed,
        out_specs=(P("ctx", "tp"), P("ctx", "tp")),
        check_vma=False,
    )
```

profile of v0, /device:TPU:416, one launch (start us, length us, event | category | flops | bytes accessed | tf_op | source)
XLA Modules:
  0.0 242.3 jit_solution(6290647112543033285)
XLA Ops:
  7.2 3.4 %collective-permute-start = (bf16[128,128]{1,0:T(8,128)(2,1)}, bf16[128,128]{1,0:T(8,128)(2,1)S(1)}, u32[]{:S(2)}, u32[]{:S(2)}) collective-permute-start(bf16[128,128]{1,0:T(8,128)(2,1)} %param.11), channel_id=1, source_target_pairs={{0,64},{8,72},{16,80},{24,88},{32,96},{40,104},{48,112},{56,120},{... | collective-permute-start | bytes 98312 | tf_op jit(solution)/shard_map/ppermute | solution.py:18
  10.6 3.3 %collective-permute-start.1 = (bf16[128,128]{1,0:T(8,128)(2,1)}, bf16[128,128]{1,0:T(8,128)(2,1)S(1)}, u32[]{:S(2)}, u32[]{:S(2)}) collective-permute-start(bf16[128,128]{1,0:T(8,128)(2,1)} %param.11), channel_id=1, source_target_pairs={{0,56},{8,64},{16,72},{24,80},{32,88},{40,96},{48,104},{56,112},{6... | collective-permute-start | bytes 98312 | tf_op jit(solution)/shard_map/ppermute | solution.py:18
  13.9 1.9 collective-permute-start.2
  15.8 2.6 %collective-permute-start.3 = (bf16[128,128]{1,0:T(8,128)(2,1)}, bf16[128,128]{1,0:T(8,128)(2,1)S(1)}, u32[]{:S(2)}, u32[]{:S(2)}) collective-permute-start(bf16[128,128]{1,0:T(8,128)(2,1)} %param.11), channel_id=1, source_target_pairs={{0,40},{8,48},{16,56},{24,64},{32,72},{40,80},{48,88},{56,96},{64,... | collective-permute-start | bytes 98312 | tf_op jit(solution)/shard_map/ppermute | solution.py:18
  18.4 2.3 collective-permute-start.4
  20.7 0.8 dynamic_slice.54
  21.5 1.4 convert_reduce_fusion
  22.9 0.8 fusion.46
  24.4 1.0 reshape_transpose_reshape.9
  25.4 2.6 %collective-permute-start.5 = (bf16[128,128]{1,0:T(8,128)(2,1)}, bf16[128,128]{1,0:T(8,128)(2,1)S(1)}, u32[]{:S(2)}, u32[]{:S(2)}) collective-permute-start(bf16[128,128]{1,0:T(8,128)(2,1)} %param.11), channel_id=1, source_target_pairs={{0,24},{8,32},{16,40},{24,48},{32,56},{40,64},{48,72},{56,80},{64,... | collective-permute-start | bytes 98312 | tf_op jit(solution)/shard_map/ppermute | solution.py:18
  28.0 3.0 %collective-permute-start.6 = (bf16[128,128]{1,0:T(8,128)(2,1)}, bf16[128,128]{1,0:T(8,128)(2,1)S(1)}, u32[]{:S(2)}, u32[]{:S(2)}) collective-permute-start(bf16[128,128]{1,0:T(8,128)(2,1)} %param.11), channel_id=1, source_target_pairs={{0,16},{8,24},{16,32},{24,40},{32,48},{40,56},{48,64},{56,72},{64,... | collective-permute-start | bytes 98312 | tf_op jit(solution)/shard_map/ppermute | solution.py:18
  31.0 1.9 collective-permute-start.7
  33.0 1.9 collective-permute-start.8
  34.9 1.9 collective-permute-start.9
  36.9 1.9 collective-permute-start.10
  38.8 1.9 collective-permute-start.11
  40.8 1.9 collective-permute-start.12
  42.7 0.8 constant_dynamic-update-slice_fusion
  43.5 3.7 %collective-permute-start.13 = (bf16[128,128]{1,0:T(8,128)(2,1)}, bf16[128,128]{1,0:T(8,128)(2,1)S(1)}, u32[]{:S(2)}, u32[]{:S(2)}) collective-permute-start(bf16[128,128]{1,0:T(8,128)(2,1)} %param.12), channel_id=1, source_target_pairs={{0,24},{8,32},{16,40},{24,48},{32,56},{40,64},{48,72},{56,80},{64,... | collective-permute-start | bytes 98312 | tf_op jit(solution)/shard_map/ppermute | solution.py:18
  47.3 3.1 %collective-permute-start.14 = (bf16[128,128]{1,0:T(8,128)(2,1)}, bf16[128,128]{1,0:T(8,128)(2,1)S(1)}, u32[]{:S(2)}, u32[]{:S(2)}) collective-permute-start(bf16[128,128]{1,0:T(8,128)(2,1)} %param.12), channel_id=1, source_target_pairs={{0,16},{8,24},{16,32},{24,40},{32,48},{40,56},{48,64},{56,72},{64,... | collective-permute-start | bytes 98312 | tf_op jit(solution)/shard_map/ppermute | solution.py:18
  50.5 1.9 collective-permute-start.15
  52.5 3.2 %collective-permute-done.14 = bf16[128,128]{1,0:T(8,128)(2,1)S(1)} collective-permute-done((bf16[128,128]{1,0:T(8,128)(2,1)}, bf16[128,128]{1,0:T(8,128)(2,1)S(1)}, u32[]{:S(2)}, u32[]{:S(2)}) %collective-permute-start.14) | collective-permute-done | bytes 32800 | tf_op jit(solution)/shard_map/ppermute | solution.py:18
  55.7 2.9 %collective-permute-done.15 = bf16[128,128]{1,0:T(8,128)(2,1)S(1)} collective-permute-done((bf16[128,128]{1,0:T(8,128)(2,1)}, bf16[128,128]{1,0:T(8,128)(2,1)S(1)}, u32[]{:S(2)}, u32[]{:S(2)}) %collective-permute-start.15) | collective-permute-done | bytes 32800 | tf_op jit(solution)/shard_map/ppermute | solution.py:18
  58.6 0.8 constant_dynamic-update-slice_fusion.9
  59.4 5.5 %while.26 = (s32[]{:T(128)}, f32[1,512]{1,0:T(1,128)S(1)}, f32[1,512]{1,0:T(1,128)S(1)}, f32[1,512,128]{2,1,0:T(8,128)S(1)}, s32[]{:T(128)}, /*index=5*/s32[1536...) while((s32[]{:T(128)}, f32[1,512]{1,0:T(1,128)S(1)}, ...), condition=%wide.region_4.5_spmd.clone, body=%wide.region_1.4_spmd.clone.sunk | while | flops 139069440 | bytes 4139747 | solution.py:103
  59.8 0.1 eq.86
  59.9 0.4 select_reduce_fusion.2
  60.3 0.3 fusion.64
  60.6 0.6 fusion.65
  61.6 0.1 eq.86
  61.7 0.4 select_reduce_fusion.2
  62.1 0.3 fusion.64
  62.4 0.6 fusion.65
  63.4 0.1 eq.86
  63.5 0.4 select_reduce_fusion.2
  63.9 0.3 fusion.64
  64.2 0.6 fusion.65
  64.9 0.1 divide_convert_fusion.2
  65.2 4.3 %fusion.48 = f32[128,4096]{1,0:T(8,128)} fusion(bf16[128,512]{1,0:T(8,128)(2,1)S(1)} %reshape_transpose_reshape.10, bf16[512,4096]{1,0:T(8,128)(2,1)} %param.13), kind=kOutput, calls=%fused_computation.94 | convolution fusion | flops 536870912 | bytes 6422528 | tf_op jit(solution)/shard_map/dot_general | solution.py:110
  69.5 0.7 all-gather.2.cloned.1.call-update
  70.2 88.7 %all-reduce.2.cloned.1.call-done = f32[128,4096]{1,0:T(8,128)} async-done(((f32[128,4096]{1,0:T(8,128)}), f32[128,4096]{1,0:T(8,128)}) %all-reduce.2.cloned.1.call-update) | async-done | bytes 2097168 | tf_op jit(solution)/shard_map/psum | solution.py:110
  159.0 32.8 %all-gather.2.cloned.1.call-done = bf16[128,4096]{1,0:T(8,128)(2,1)} async-done(((bf16[128,512]{1,0:T(8,128)(2,1)}), bf16[128,4096]{1,0:T(8,128)(2,1)}) %all-gather.2.cloned.1.call-update) | async-done | bytes 1048592 | tf_op jit(solution)/shard_map/all_gather | solution.py:111
  191.8 5.3 %fusion.43 = (bf16[128,512]{1,0:T(8,128)(2,1)S(1)}, bf16[128,512]{1,0:T(8,128)(2,1)}) fusion(bf16[128,512]{1,0:T(8,128)(2,1)S(1)} %reshape_transpose_reshape.10, bf16[512,4096]{1,0:T(8,128)(2,1)} %param.13, f32[128,4096]{1,0:T(8,128)} %all-reduce.2.cloned.1.call-done, bf16[128,4096]{1,0:T(8,128)(2,1)} %all-gather.2.cloned.1.call-done), kind=kOutput, calls=%fused_computation.56 | convolution fusion | flops 540540928 | bytes 7733248 | tf_op jit(solution)/shard_map/dot_general | solution.py:113
  197.2 3.8 %while.27 = (s32[]{:T(128)}, f32[1,1536]{1,0:T(1,128)S(1)}, s32[]{:T(128)}, s32[1536]{0:T(1024)S(1)}, s32[]{:T(128)}, /*index=5*/bf16[1536,1,128]{2,0,1:T(8,128)...) while((s32[]{:T(128)}, f32[1,1536]{1,0:T(1,128)S(1)}, ...), condition=%wide.region_8.9_spmd.clone, body=%wide.region_6.8_spmd.clone.sunk | while | flops 136578048 | bytes 2661103 | solution.py:134
  197.5 0.1 eq.90
  197.6 0.5 fusion.70
  198.1 0.3 fusion.71
  198.8 0.1 eq.90
  198.9 0.5 fusion.70
  199.4 0.3 fusion.71
  200.1 0.1 eq.90
  200.2 0.5 fusion.70
  200.7 0.3 fusion.71
  201.1 5.5 %collective-permute-start.16 = (f32[1,128]{1,0:T(1,128)S(1)}, f32[1,128]{1,0:T(1,128)S(1)}, u32[]{:S(2)}, u32[]{:S(2)}) collective-permute-start(f32[1,128]{1,0:T(1,128)S(1)} %get-tuple-element.257), channel_id=1, source_target_pairs={{8,0},{16,8},{24,16},{32,24},{40,32},{48,40},{56,48},{64,56},{72,6... | collective-permute-start | bytes 1544 | tf_op jit(solution)/shard_map/ppermute | solution.py:18
  206.5 2.7 %collective-permute-start.17 = (f32[1,128]{1,0:T(1,128)S(1)}, f32[1,128]{1,0:T(1,128)S(1)}, u32[]{:S(2)}, u32[]{:S(2)}) collective-permute-start(f32[1,128]{1,0:T(1,128)S(1)} %get-tuple-element.263), channel_id=1, source_target_pairs={{16,0},{24,8},{32,16},{40,24},{48,32},{56,40},{64,48},{72,56},{80,... | collective-permute-start | bytes 1544 | tf_op jit(solution)/shard_map/ppermute | solution.py:18
  209.3 3.5 %collective-permute-start.18 = (f32[1,128]{1,0:T(1,128)S(1)}, f32[1,128]{1,0:T(1,128)S(1)}, u32[]{:S(2)}, u32[]{:S(2)}) collective-permute-start(f32[1,128]{1,0:T(1,128)S(1)} %get-tuple-element.262), channel_id=1, source_target_pairs={{24,0},{32,8},{40,16},{48,24},{56,32},{64,40},{72,48},{80,56},{88,... | collective-permute-start | bytes 1544 | tf_op jit(solution)/shard_map/ppermute | solution.py:18
  212.8 4.5 %collective-permute-start.19 = (f32[1,128]{1,0:T(1,128)S(1)}, f32[1,128]{1,0:T(1,128)S(1)}, u32[]{:S(2)}, u32[]{:S(2)}) collective-permute-start(f32[1,128]{1,0:T(1,128)S(1)} %get-tuple-element.261), channel_id=1, source_target_pairs={{32,0},{40,8},{48,16},{56,24},{64,32},{72,40},{80,48},{88,56},{96,... | collective-permute-start | bytes 1544 | tf_op jit(solution)/shard_map/ppermute | solution.py:18
  217.4 4.3 %collective-permute-start.20 = (f32[1,128]{1,0:T(1,128)S(1)}, f32[1,128]{1,0:T(1,128)S(1)}, u32[]{:S(2)}, u32[]{:S(2)}) collective-permute-start(f32[1,128]{1,0:T(1,128)S(1)} %get-tuple-element.260), channel_id=1, source_target_pairs={{40,0},{48,8},{56,16},{64,24},{72,32},{80,40},{88,48},{96,56},{104... | collective-permute-start | bytes 1544 | tf_op jit(solution)/shard_map/ppermute | solution.py:18
  221.7 4.9 %collective-permute-start.21 = (f32[1,128]{1,0:T(1,128)S(1)}, f32[1,128]{1,0:T(1,128)S(1)}, u32[]{:S(2)}, u32[]{:S(2)}) collective-permute-start(f32[1,128]{1,0:T(1,128)S(1)} %get-tuple-element.259), channel_id=1, source_target_pairs={{48,0},{56,8},{64,16},{72,24},{80,32},{88,40},{96,48},{104,56},{11... | collective-permute-start | bytes 1544 | tf_op jit(solution)/shard_map/ppermute | solution.py:18
  226.6 1.9 collective-permute-start.22
  228.6 2.3 collective-permute-start.23
  230.9 3.3 %collective-permute-done.22 = f32[1,128]{1,0:T(1,128)S(1)} collective-permute-done((f32[1,128]{1,0:T(1,128)S(1)}, f32[1,128]{1,0:T(1,128)S(1)}, u32[]{:S(2)}, u32[]{:S(2)}) %collective-permute-start.22) | collective-permute-done | bytes 544 | tf_op jit(solution)/shard_map/ppermute | solution.py:18
  234.2 0.7 collective-permute-done.23
  234.9 0.5 add_bitcast_fusion
  (91 shorter events, 2.3 us)
Async XLA Ops:
  7.2 151.8 %all-reduce.2.cloned.1.call-start = ((), (), s32[]{:S(2)}) async-start(), calls=%async_computation.1 | async-start | bytes 4194304 | tf_op jit(solution)/shard_map/psum | solution.py:110
  7.2 18.2 %collective-permute-start = (bf16[128,128]{1,0:T(8,128)(2,1)}, bf16[128,128]{1,0:T(8,128)(2,1)S(1)}, u32[]{:S(2)}, u32[]{:S(2)}) collective-permute-start(bf16[128,128]{1,0:T(8,128)(2,1)} %param.11), channel_id=1, source_target_pairs={{0,64},{8,72},{16,80},{24,88},{32,96},{40,104},{48,112},{56,120},{... | collective-permute-start | bytes 98312 | tf_op jit(solution)/shard_map/ppermute | solution.py:18
  10.6 17.4 %collective-permute-start.1 = (bf16[128,128]{1,0:T(8,128)(2,1)}, bf16[128,128]{1,0:T(8,128)(2,1)S(1)}, u32[]{:S(2)}, u32[]{:S(2)}) collective-permute-start(bf16[128,128]{1,0:T(8,128)(2,1)} %param.11), channel_id=1, source_target_pairs={{0,56},{8,64},{16,72},{24,80},{32,88},{40,96},{48,104},{56,112},{6... | collective-permute-start | bytes 98312 | tf_op jit(solution)/shard_map/ppermute | solution.py:18
  13.9 17.1 %collective-permute-start.2 = (bf16[128,128]{1,0:T(8,128)(2,1)}, bf16[128,128]{1,0:T(8,128)(2,1)S(1)}, u32[]{:S(2)}, u32[]{:S(2)}) collective-permute-start(bf16[128,128]{1,0:T(8,128)(2,1)} %param.11), channel_id=1, source_target_pairs={{0,48},{8,56},{16,64},{24,72},{32,80},{40,88},{48,96},{56,104},{64... | collective-permute-start | bytes 98312 | tf_op jit(solution)/shard_map/ppermute | solution.py:18
  15.8 17.1 %collective-permute-start.3 = (bf16[128,128]{1,0:T(8,128)(2,1)}, bf16[128,128]{1,0:T(8,128)(2,1)S(1)}, u32[]{:S(2)}, u32[]{:S(2)}) collective-permute-start(bf16[128,128]{1,0:T(8,128)(2,1)} %param.11), channel_id=1, source_target_pairs={{0,40},{8,48},{16,56},{24,64},{32,72},{40,80},{48,88},{56,96},{64,... | collective-permute-start | bytes 98312 | tf_op jit(solution)/shard_map/ppermute | solution.py:18
  18.4 16.5 %collective-permute-start.4 = (bf16[128,128]{1,0:T(8,128)(2,1)}, bf16[128,128]{1,0:T(8,128)(2,1)S(1)}, u32[]{:S(2)}, u32[]{:S(2)}) collective-permute-start(bf16[128,128]{1,0:T(8,128)(2,1)} %param.11), channel_id=1, source_target_pairs={{0,32},{8,40},{16,48},{24,56},{32,64},{40,72},{48,80},{56,88},{64,... | collective-permute-start | bytes 98312 | tf_op jit(solution)/shard_map/ppermute | solution.py:18
  25.4 11.5 %collective-permute-start.5 = (bf16[128,128]{1,0:T(8,128)(2,1)}, bf16[128,128]{1,0:T(8,128)(2,1)S(1)}, u32[]{:S(2)}, u32[]{:S(2)}) collective-permute-start(bf16[128,128]{1,0:T(8,128)(2,1)} %param.11), channel_id=1, source_target_pairs={{0,24},{8,32},{16,40},{24,48},{32,56},{40,64},{48,72},{56,80},{64,... | collective-permute-start | bytes 98312 | tf_op jit(solution)/shard_map/ppermute | solution.py:18
  28.0 10.9 %collective-permute-start.6 = (bf16[128,128]{1,0:T(8,128)(2,1)}, bf16[128,128]{1,0:T(8,128)(2,1)S(1)}, u32[]{:S(2)}, u32[]{:S(2)}) collective-permute-start(bf16[128,128]{1,0:T(8,128)(2,1)} %param.11), channel_id=1, source_target_pairs={{0,16},{8,24},{16,32},{24,40},{32,48},{40,56},{48,64},{56,72},{64,... | collective-permute-start | bytes 98312 | tf_op jit(solution)/shard_map/ppermute | solution.py:18
  31.0 9.8 %collective-permute-start.7 = (bf16[128,128]{1,0:T(8,128)(2,1)}, bf16[128,128]{1,0:T(8,128)(2,1)S(1)}, u32[]{:S(2)}, u32[]{:S(2)}) collective-permute-start(bf16[128,128]{1,0:T(8,128)(2,1)} %param.11), channel_id=1, source_target_pairs={{0,8},{8,16},{16,24},{24,32},{32,40},{40,48},{48,56},{56,64},{64,7... | collective-permute-start | bytes 98312 | tf_op jit(solution)/shard_map/ppermute | solution.py:18
  33.0 10.6 %collective-permute-start.8 = (bf16[128,128]{1,0:T(8,128)(2,1)}, bf16[128,128]{1,0:T(8,128)(2,1)S(1)}, u32[]{:S(2)}, u32[]{:S(2)}) collective-permute-start(bf16[128,128]{1,0:T(8,128)(2,1)} %param.12), channel_id=1, source_target_pairs={{0,64},{8,72},{16,80},{24,88},{32,96},{40,104},{48,112},{56,120},{... | collective-permute-start | bytes 98312 | tf_op jit(solution)/shard_map/ppermute | solution.py:18
  34.9 12.4 %collective-permute-start.9 = (bf16[128,128]{1,0:T(8,128)(2,1)}, bf16[128,128]{1,0:T(8,128)(2,1)S(1)}, u32[]{:S(2)}, u32[]{:S(2)}) collective-permute-start(bf16[128,128]{1,0:T(8,128)(2,1)} %param.12), channel_id=1, source_target_pairs={{0,56},{8,64},{16,72},{24,80},{32,88},{40,96},{48,104},{56,112},{6... | collective-permute-start | bytes 98312 | tf_op jit(solution)/shard_map/ppermute | solution.py:18
  36.9 13.6 %collective-permute-start.10 = (bf16[128,128]{1,0:T(8,128)(2,1)}, bf16[128,128]{1,0:T(8,128)(2,1)S(1)}, u32[]{:S(2)}, u32[]{:S(2)}) collective-permute-start(bf16[128,128]{1,0:T(8,128)(2,1)} %param.12), channel_id=1, source_target_pairs={{0,48},{8,56},{16,64},{24,72},{32,80},{40,88},{48,96},{56,104},{64... | collective-permute-start | bytes 98312 | tf_op jit(solution)/shard_map/ppermute | solution.py:18
  38.8 13.6 %collective-permute-start.11 = (bf16[128,128]{1,0:T(8,128)(2,1)}, bf16[128,128]{1,0:T(8,128)(2,1)S(1)}, u32[]{:S(2)}, u32[]{:S(2)}) collective-permute-start(bf16[128,128]{1,0:T(8,128)(2,1)} %param.12), channel_id=1, source_target_pairs={{0,40},{8,48},{16,56},{24,64},{32,72},{40,80},{48,88},{56,96},{64,... | collective-permute-start | bytes 98312 | tf_op jit(solution)/shard_map/ppermute | solution.py:18
  40.8 11.7 %collective-permute-start.12 = (bf16[128,128]{1,0:T(8,128)(2,1)}, bf16[128,128]{1,0:T(8,128)(2,1)S(1)}, u32[]{:S(2)}, u32[]{:S(2)}) collective-permute-start(bf16[128,128]{1,0:T(8,128)(2,1)} %param.12), channel_id=1, source_target_pairs={{0,32},{8,40},{16,48},{24,56},{32,64},{40,72},{48,80},{56,88},{64,... | collective-permute-start | bytes 98312 | tf_op jit(solution)/shard_map/ppermute | solution.py:18
  43.5 8.9 %collective-permute-start.13 = (bf16[128,128]{1,0:T(8,128)(2,1)}, bf16[128,128]{1,0:T(8,128)(2,1)S(1)}, u32[]{:S(2)}, u32[]{:S(2)}) collective-permute-start(bf16[128,128]{1,0:T(8,128)(2,1)} %param.12), channel_id=1, source_target_pairs={{0,24},{8,32},{16,40},{24,48},{32,56},{40,64},{48,72},{56,80},{64,... | collective-permute-start | bytes 98312 | tf_op jit(solution)/shard_map/ppermute | solution.py:18
  47.3 8.4 %collective-permute-start.14 = (bf16[128,128]{1,0:T(8,128)(2,1)}, bf16[128,128]{1,0:T(8,128)(2,1)S(1)}, u32[]{:S(2)}, u32[]{:S(2)}) collective-permute-start(bf16[128,128]{1,0:T(8,128)(2,1)} %param.12), channel_id=1, source_target_pairs={{0,16},{8,24},{16,32},{24,40},{32,48},{40,56},{48,64},{56,72},{64,... | collective-permute-start | bytes 98312 | tf_op jit(solution)/shard_map/ppermute | solution.py:18
  50.5 8.1 %collective-permute-start.15 = (bf16[128,128]{1,0:T(8,128)(2,1)}, bf16[128,128]{1,0:T(8,128)(2,1)S(1)}, u32[]{:S(2)}, u32[]{:S(2)}) collective-permute-start(bf16[128,128]{1,0:T(8,128)(2,1)} %param.12), channel_id=1, source_target_pairs={{0,8},{8,16},{16,24},{24,32},{32,40},{40,48},{48,56},{56,64},{64,7... | collective-permute-start | bytes 98312 | tf_op jit(solution)/shard_map/ppermute | solution.py:18
  69.4 122.3 %all-gather.2.cloned.1.call-start = ((), (), s32[]{:S(2)}) async-start(), calls=%async_computation | async-start | bytes 1179648 | tf_op jit(solution)/shard_map/all_gather | solution.py:111
  201.1 20.6 %collective-permute-start.16 = (f32[1,128]{1,0:T(1,128)S(1)}, f32[1,128]{1,0:T(1,128)S(1)}, u32[]{:S(2)}, u32[]{:S(2)}) collective-permute-start(f32[1,128]{1,0:T(1,128)S(1)} %get-tuple-element.257), channel_id=1, source_target_pairs={{8,0},{16,8},{24,16},{32,24},{40,32},{48,40},{56,48},{64,56},{72,6... | collective-permute-start | bytes 1544 | tf_op jit(solution)/shard_map/ppermute | solution.py:18
  206.5 20.1 %collective-permute-start.17 = (f32[1,128]{1,0:T(1,128)S(1)}, f32[1,128]{1,0:T(1,128)S(1)}, u32[]{:S(2)}, u32[]{:S(2)}) collective-permute-start(f32[1,128]{1,0:T(1,128)S(1)} %get-tuple-element.263), channel_id=1, source_target_pairs={{16,0},{24,8},{32,16},{40,24},{48,32},{56,40},{64,48},{72,56},{80,... | collective-permute-start | bytes 1544 | tf_op jit(solution)/shard_map/ppermute | solution.py:18
  209.3 19.3 %collective-permute-start.18 = (f32[1,128]{1,0:T(1,128)S(1)}, f32[1,128]{1,0:T(1,128)S(1)}, u32[]{:S(2)}, u32[]{:S(2)}) collective-permute-start(f32[1,128]{1,0:T(1,128)S(1)} %get-tuple-element.262), channel_id=1, source_target_pairs={{24,0},{32,8},{40,16},{48,24},{56,32},{64,40},{72,48},{80,56},{88,... | collective-permute-start | bytes 1544 | tf_op jit(solution)/shard_map/ppermute | solution.py:18
  212.8 18.0 %collective-permute-start.19 = (f32[1,128]{1,0:T(1,128)S(1)}, f32[1,128]{1,0:T(1,128)S(1)}, u32[]{:S(2)}, u32[]{:S(2)}) collective-permute-start(f32[1,128]{1,0:T(1,128)S(1)} %get-tuple-element.261), channel_id=1, source_target_pairs={{32,0},{40,8},{48,16},{56,24},{64,32},{72,40},{80,48},{88,56},{96,... | collective-permute-start | bytes 1544 | tf_op jit(solution)/shard_map/ppermute | solution.py:18
  217.4 13.5 %collective-permute-start.20 = (f32[1,128]{1,0:T(1,128)S(1)}, f32[1,128]{1,0:T(1,128)S(1)}, u32[]{:S(2)}, u32[]{:S(2)}) collective-permute-start(f32[1,128]{1,0:T(1,128)S(1)} %get-tuple-element.260), channel_id=1, source_target_pairs={{40,0},{48,8},{56,16},{64,24},{72,32},{80,40},{88,48},{96,56},{104... | collective-permute-start | bytes 1544 | tf_op jit(solution)/shard_map/ppermute | solution.py:18
  221.7 9.2 %collective-permute-start.21 = (f32[1,128]{1,0:T(1,128)S(1)}, f32[1,128]{1,0:T(1,128)S(1)}, u32[]{:S(2)}, u32[]{:S(2)}) collective-permute-start(f32[1,128]{1,0:T(1,128)S(1)} %get-tuple-element.259), channel_id=1, source_target_pairs={{48,0},{56,8},{64,16},{72,24},{80,32},{88,40},{96,48},{104,56},{11... | collective-permute-start | bytes 1544 | tf_op jit(solution)/shard_map/ppermute | solution.py:18
  226.6 7.6 %collective-permute-start.22 = (f32[1,128]{1,0:T(1,128)S(1)}, f32[1,128]{1,0:T(1,128)S(1)}, u32[]{:S(2)}, u32[]{:S(2)}) collective-permute-start(f32[1,128]{1,0:T(1,128)S(1)} %get-tuple-element.258), channel_id=1, source_target_pairs={{56,0},{64,8},{72,16},{80,24},{88,32},{96,40},{104,48},{112,56},{1... | collective-permute-start | bytes 1544 | tf_op jit(solution)/shard_map/ppermute | solution.py:18
  228.6 6.4 %collective-permute-start.23 = (f32[1,128]{1,0:T(1,128)S(1)}, f32[1,128]{1,0:T(1,128)S(1)}, u32[]{:S(2)}, u32[]{:S(2)}) collective-permute-start(f32[1,128]{1,0:T(1,128)S(1)} %get-tuple-element.264), channel_id=1, source_target_pairs={{64,0},{72,8},{80,16},{88,24},{96,32},{104,40},{112,48},{120,56},{... | collective-permute-start | bytes 1544 | tf_op jit(solution)/shard_map/ppermute | solution.py:18
Sparse Core Ops, SparseCore 0:
  69.6 89.3 all-reduce.1
  161.1 30.5 all-gather.1
where the time goes:
time: 243 us; the launch traced here: 242 us
  waiting for transfers between devices  132 us (54%)
  starting transfers between devices  69.1 us (28%)
  between operations  15.3 us (6%)
  matrix products  15.2 us (6%)
  local copies, waits for them, and re-layouts  5.97 us (2%)
  other arithmetic  4.04 us (2%)
    psum x1, waiting for transfers between devices, on_device(): lax.psum(jnp.dot(attention, w_out, preferred_element_type=jnp.float32), '...  88.7 us
    ppermute x24, starting transfers between devices, passed_along(): return lax.ppermute(shard, axis, pairs)  69 us
    all_gather x1, waiting for transfers between devices, on_device(): lax.all_gather(relevance_out, 'tp', axis=1, tiled=True).astype(jnp.float32)  32.8 us
    ppermute x24, waiting for transfers between devices, passed_along(): return lax.ppermute(shard, axis, pairs)  10.2 us
    dot_general x1, matrix products, on_device(): lax.dot_general(ratio, w_out, (((1,), (1,)), ((), ())), preferred_element...  5.35 us
  transfers between devices with their start and end apart: 26, of which 6 were waited for; matrix products, arithmetic and copies ran while one was open for 2% of the time, Pallas kernels for 0%

commit v1 on v0

v1 whole, which is shorter than its diff:
```python
import jax
import jax.numpy as jnp
from jax import lax
from jax.experimental import pallas as pl
from jax.experimental.pallas import tpu as pltpu
from jax.sharding import PartitionSpec as P

MESH = pl.DeviceIdType.MESH
HEAD_DIM = 128
GROUP = 4
TOKENS = 128
ROWS = TOKENS * GROUP
SLOTS = 9
CTX = 64
XS = 4
FEAT = 512
HALF = TOKENS // 2
BF = jnp.bfloat16
F32 = jnp.float32
MASKED = -1e30
SCALE2 = HEAD_DIM ** (-0.5) * 1.4426950408889634


def dot_nt(a, b):
    return lax.dot_general(a, b, (((1,), (1,)), ((), ())), preferred_element_type=F32)


def dot_nn(a, b):
    return jnp.dot(a, b, preferred_element_type=F32)


def kernel(
    q_hbm, k_hbm, v_hbm, w_hbm, rel_hbm, seg_hbm, heads_hbm, tokens_ref,
    q, kv, w, rel, seg, score, weight, peak, att, send_two, from_far_left, from_far_right,
    merged_right, merged_left, direct_right, direct_left, in_left, in_right,
    ratio, cross_out, cross_in, heads, passed, inverse, term_out, term_in,
    local_sem, w_local_sem, w_send, w_recv, kv_send, kv_recv, a_send, a_recv,
    rs_send, rs_recv, ag_send, ag_recv, c_send, c_recv, t_send, t_recv,
):
    me = lax.axis_index("ctx")
    tp = lax.axis_index("tp")
    y = lax.rem(me, 4)
    core = lax.rem(tp, 2)
    x = lax.div(tp, 2)
    base = me - y
    y_right = base + lax.rem(y + 1, 4)
    y_left = base + lax.rem(y + 3, 4)
    up = lax.rem(me + 4, CTX)
    other = 1 - core
    partner = x * 2 + other
    x_right_i = lax.rem(x + 1, XS)
    x_left_i = lax.rem(x + 3, XS)
    x_far_i = lax.rem(x + 2, XS)
    x_right = x_right_i * 2 + core
    x_left = x_left_i * 2 + core

    def remote(src, dst, send, recv, ctx, tpi):
        return pltpu.make_async_remote_copy(
            src_ref=src, dst_ref=dst, send_sem=send, recv_sem=recv,
            device_id=(ctx, tpi), device_id_type=MESH,
        )

    loads = [
        pltpu.make_async_copy(k_hbm, kv.at[0, 0], local_sem.at[0]),
        pltpu.make_async_copy(v_hbm, kv.at[0, 1], local_sem.at[1]),
        pltpu.make_async_copy(seg_hbm, seg, local_sem.at[2]),
    ]
    for h in range(GROUP):
        loads.append(
            pltpu.make_async_copy(
                q_hbm.at[:, h * HEAD_DIM:(h + 1) * HEAD_DIM],
                q.at[h * TOKENS:(h + 1) * TOKENS, :],
                local_sem.at[3 + h],
            )
        )
    loads.append(pltpu.make_async_copy(rel_hbm, rel, local_sem.at[7]))
    for load in loads:
        load.start()

    barrier = pltpu.get_barrier_semaphore()

    def greet(ctx, tpi):
        pl.semaphore_signal(barrier, inc=1, device_id=(ctx, tpi), device_id_type=MESH)

    greet(me, partner)
    greet(me, x_right)
    greet(me, x_left)
    for d in range(1, SLOTS):
        greet(lax.rem(me + d, CTX), tp)
        greet(lax.rem(me + CTX - d, CTX), tp)
    pl.semaphore_wait(barrier, 19)

    def kv_copy(number, half, src, dst, ctx):
        return remote(
            kv.at[src, half], kv.at[dst, half], kv_send.at[number, half], kv_recv.at[dst, half], ctx, tp
        )

    def arrive(slot, half):
        remote(
            kv.at[slot, half], kv.at[slot, half], kv_send.at[0, half], kv_recv.at[slot, half], me, tp
        ).wait_recv()

    right_src = jnp.where(y < 3, 0, 8)
    right_dst = jnp.where(y < 3, 1, 5)
    left_src = jnp.where(y > 0, 8, 0)
    left_dst = jnp.where(y > 0, 7, 3)
    next_right_dst = jnp.where(y < 3, 5, 1)
    next_left_dst = jnp.where(y > 0, 3, 7)
    relay_right_src = jnp.where(y < 3, 1, 5)
    relay_left_src = jnp.where(y > 0, 7, 3)

    def up_one(half):
        return kv_copy(0, half, 0, 4, up)

    def up_two(half):
        return kv_copy(1, half, 4, 8, up)

    def right_zero(half):
        return kv_copy(2, half, right_src, right_dst, y_right)

    def left_zero(half):
        return kv_copy(3, half, left_src, left_dst, y_left)

    def right_one(half):
        return kv_copy(4, half, 4, next_right_dst, y_right)

    def left_one(half):
        return kv_copy(5, half, 4, next_left_dst, y_left)

    def relay_right(half):
        return kv_copy(6, half, relay_right_src, 2, y_right)

    def relay_left(half):
        return kv_copy(7, half, relay_left_src, 6, y_left)

    loads[0].wait()
    up_one(0).start()
    loads[1].wait()
    up_one(1).start()

    @pl.when(y < 3)
    def _():
        right_zero(0).start()
        right_zero(1).start()

    @pl.when(y == 0)
    def _():
        left_zero(0).start()
        left_zero(1).start()

    w_copies = []
    for i in range(XS):
        w_copies.append(
            pltpu.make_async_copy(
                w_hbm.at[:, pl.ds(pl.multiple_of((2 * i + core) * FEAT, FEAT), FEAT)],
                w.at[core, i], w_local_sem.at[i],
            )
        )
        w_copies.append(
            remote(
                w_hbm.at[:, pl.ds(pl.multiple_of((2 * i + other) * FEAT, FEAT), FEAT)],
                w.at[core, i], w_send.at[i], w_recv.at[i], me, partner,
            )
        )
    for copy in w_copies:
        copy.start()

    for load in loads[2:]:
        load.wait()

    own_seg = jnp.broadcast_to(seg[pl.ds(me, 1), :].astype(F32), (TOKENS, TOKENS)).T
    row_at = lax.broadcasted_iota(jnp.int32, (TOKENS, TOKENS), 0)
    key_at = lax.broadcasted_iota(jnp.int32, (TOKENS, TOKENS), 1)

    def score_block(slot, first=False):
        key_seg = seg[pl.ds(lax.rem(me + CTX - slot, CTX), 1), :].astype(F32)
        visible = own_seg == key_seg
        if first:
            visible = visible & (key_at <= row_at)
        for h in range(GROUP):
            rows = pl.ds(h * TOKENS, TOKENS)
            s = dot_nt(q[rows, :], kv[slot, 0])
            s = jnp.where(visible, s, MASKED)
            score[slot, rows, :] = s
            if first:
                peak[rows, :] = s
            else:
                peak[rows, :] = jnp.maximum(peak[rows, :], s)

    score_block(0, True)

    for half in range(2):
        arrive(4, half)
        up_two(half).start()
        right_one(half).start()
        left_one(half).start()
    score_block(4)

    inner_y = (y == 1) | (y == 2)
    outer_y = (y == 0) | (y == 3)

    @pl.when(y > 0)
    def _():
        for half in range(2):
            arrive(1, half)

            @pl.when(y < 3)
            def _():
                relay_right(half).start()

    @pl.when(y == 3)
    def _():
        for half in range(2):
            arrive(3, half)

    for half in range(2):
        arrive(8, half)

        @pl.when(y > 0)
        def _():
            left_zero(half).start()

        @pl.when(y == 3)
        def _():
            right_zero(half).start()

    score_block(jnp.where(y > 0, 1, 8))

    one_left = jnp.where(y > 0, 5, 1)
    one_right = jnp.where(y < 3, 3, 7)
    for half in range(2):
        arrive(one_left, half)

        @pl.when(outer_y)
        def _():
            relay_right(half).start()

        arrive(one_right, half)

        @pl.when(outer_y)
        def _():
            relay_left(half).start()

    score_block(jnp.where(y > 0, 8, 1))
    score_block(5 - jnp.where(y > 0, 0, 2))
    @pl.when(y == 0)
    def _():
        for half in range(2):
            arrive(5, half)

    @pl.when(y < 3)
    def _():
        for half in range(2):
            arrive(7, half)

            @pl.when(inner_y)
            def _():
                relay_left(half).start()

    score_block(jnp.where(y > 0, 3, 5))
    score_block(7)
    for half in range(2):
        arrive(2, half)
    score_block(2)
    for half in range(2):
        arrive(6, half)
    score_block(6)

    values = kv[:, 1].reshape(SLOTS * TOKENS, HEAD_DIM)
    for h in range(GROUP):
        rows = pl.ds(h * TOKENS, TOKENS)
        top = jnp.max(peak[rows, :], axis=1, keepdims=True)
        top = jnp.broadcast_to(top, (TOKENS, TOKENS))
        total = jnp.zeros((TOKENS, TOKENS), F32)
        for slot in range(SLOTS):
            e = jnp.exp2((score[slot, rows, :] - top) * SCALE2)
            total = total + e
            score[slot, rows, :] = e
            weight[rows, slot * TOKENS:(slot + 1) * TOKENS] = e.astype(BF)
        inv = 1.0 / jnp.broadcast_to(jnp.sum(total, axis=1, keepdims=True), (TOKENS, TOKENS))
        columns = slice(h * HEAD_DIM, (h + 1) * HEAD_DIM)
        inverse[:, columns] = inv
        summed = dot_nn(weight[rows, :], values)
        att[core, :, columns] = (summed * inv).astype(BF)

    a_copy = remote(att.at[core], att.at[core], a_send, a_recv, me, partner)
    a_copy.start()
    for copy in w_copies[0::2]:
        copy.wait()
    for copy in w_copies[1::2]:
        copy.wait_recv()
    remote(att.at[other], att.at[other], a_send, a_recv, me, partner).wait_recv()

    def project(i):
        return dot_nn(att[core], w[core, i]) + dot_nn(att[other], w[other, i])

    def rs(number, src, dst, tpi):
        return remote(src, dst, rs_send.at[number], rs_recv.at[number], me, tpi)

    send_two[...] = project(x_far_i).astype(BF)
    top_rows, low_rows = pl.ds(0, HALF), pl.ds(HALF, HALF)
    far_right = rs(0, send_two.at[top_rows], from_far_left, x_right)
    far_left = rs(1, send_two.at[low_rows], from_far_right, x_left)
    far_right.start()
    far_left.start()
    to_right = project(x_right_i)
    direct_right[...] = to_right[HALF:].astype(BF)
    near_right = rs(2, direct_right, in_left.at[low_rows], x_right)
    near_right.start()
    to_left = project(x_left_i)
    direct_left[...] = to_left[:HALF].astype(BF)
    near_left = rs(3, direct_left, in_right.at[top_rows], x_left)
    near_left.start()
    far_right.wait_recv()
    merged_right[...] = (to_right[:HALF] + from_far_left[...].astype(F32)).astype(BF)
    last_right = rs(4, merged_right, in_left.at[top_rows], x_right)
    last_right.start()
    far_left.wait_recv()
    merged_left[...] = (to_left[HALF:] + from_far_right[...].astype(F32)).astype(BF)
    last_left = rs(5, merged_left, in_right.at[low_rows], x_left)
    last_left.start()
    mine = project(x)
    for copy in (near_right, near_left, last_right, last_left):
        copy.wait_recv()

    total = mine + in_left[...].astype(F32) + in_right[...].astype(F32)
    ratio[x] = (rel[...].astype(F32) * total / (total * total + 1.0)).astype(BF)

    def ag(number, owner, rows, tpi):
        return remote(
            ratio.at[owner, rows], ratio.at[owner, rows], ag_send.at[number], ag_recv.at[number], me, tpi
        )

    shares = [
        ag(0, x, top_rows, x_right), ag(1, x, low_rows, x_left),
        ag(2, x, low_rows, x_right), ag(3, x, top_rows, x_left),
    ]
    for copy in shares:
        copy.start()
    back_other = dot_nt(ratio[x], w[other, x])
    back_own = dot_nt(ratio[x], w[core, x])
    ag(0, x_left_i, top_rows, x_right).wait_recv()
    pass_right = ag(4, x_left_i, top_rows, x_right)
    pass_right.start()
    ag(1, x_right_i, low_rows, x_left).wait_recv()
    pass_left = ag(5, x_right_i, low_rows, x_left)
    pass_left.start()
    ag(2, x_left_i, low_rows, x_right).wait_recv()
    back_other += dot_nt(ratio[x_left_i], w[other, x_left_i])
    back_own += dot_nt(ratio[x_left_i], w[core, x_left_i])
    ag(3, x_right_i, top_rows, x_left).wait_recv()
    back_other += dot_nt(ratio[x_right_i], w[other, x_right_i])
    back_own += dot_nt(ratio[x_right_i], w[core, x_right_i])
    ag(4, x_far_i, top_rows, x_right).wait_recv()
    ag(5, x_far_i, low_rows, x_left).wait_recv()
    back_other += dot_nt(ratio[x_far_i], w[other, x_far_i])
    cross_out[...] = back_other.astype(BF)
    cross = remote(cross_out, cross_in, c_send, c_recv, me, partner)
    cross.start()
    back_own += dot_nt(ratio[x_far_i], w[core, x_far_i])
    cross.wait_recv()
    a = att[core].astype(F32)
    carried = a * (back_own + cross_in[...].astype(F32))
    heads[...] = carried.astype(BF)
    heads_copy = pltpu.make_async_copy(heads, heads_hbm, local_sem.at[0])
    heads_copy.start()
    scaled = carried * a / (a * a + 1.0) * inverse[...]
    for h in range(GROUP):
        passed[h * TOKENS:(h + 1) * TOKENS, :] = scaled[:, h * HEAD_DIM:(h + 1) * HEAD_DIM].astype(BF)

    def term(slot):
        inner = dot_nt(passed[...], kv[slot, 1])
        return jnp.sum(score[slot] * inner, axis=0, keepdims=True)

    def term_copy(slot):
        return remote(
            term_out.at[slot], term_in.at[slot], t_send.at[slot], t_recv.at[slot],
            lax.rem(me + CTX - slot, CTX), tp,
        )

    for slot in range(SLOTS - 1, 0, -1):
        term_out[slot] = term(slot)
        term_copy(slot).start()
    own = term(0)
    for slot in range(1, SLOTS):
        term_copy(slot).wait_recv()
        own = own + term_in[slot]
    tokens_ref[...] = jnp.broadcast_to(own, (TOKENS, TOKENS)).T[:, 0:1]

    heads_copy.wait()
    for copy in w_copies[1::2]:
        copy.wait_send()
    for half in range(2):
        for make in (up_one, up_two, right_zero, left_zero, right_one, left_one, relay_right, relay_left):
            make(half).wait_send()
    a_copy.wait_send()
    for copy in (far_right, far_left, near_right, near_left, last_right, last_left):
        copy.wait_send()
    for copy in shares + [pass_right, pass_left]:
        copy.wait_send()
    cross.wait_send()
    for slot in range(1, SLOTS):
        term_copy(slot).wait_send()


def on_device(queries, keys, values, w_out, relevance_out, segment_ids):
    anywhere = pl.BlockSpec(memory_space=pl.ANY)
    vmem, dma = pltpu.VMEM, pltpu.SemaphoreType.DMA
    return pl.pallas_call(
        kernel,
        out_shape=(
            jax.ShapeDtypeStruct((TOKENS, GROUP * HEAD_DIM), BF),
            jax.ShapeDtypeStruct((TOKENS, 1), F32),
        ),
        in_specs=[anywhere] * 6,
        out_specs=(anywhere, pl.BlockSpec(memory_space=pltpu.VMEM)),
        scratch_shapes=[
            vmem((ROWS, HEAD_DIM), BF),
            vmem((SLOTS, 2, TOKENS, HEAD_DIM), BF),
            vmem((2, XS, FEAT, FEAT), BF),
            vmem((TOKENS, FEAT), BF),
            vmem((CTX, TOKENS), jnp.int32),
            vmem((SLOTS, ROWS, TOKENS), F32),
            vmem((ROWS, SLOTS * TOKENS), BF),
            vmem((ROWS, TOKENS), F32),
            vmem((2, TOKENS, FEAT), BF),
            vmem((TOKENS, FEAT), BF),
            vmem((HALF, FEAT), BF),
            vmem((HALF, FEAT), BF),
            vmem((HALF, FEAT), BF),
            vmem((HALF, FEAT), BF),
            vmem((HALF, FEAT), BF),
            vmem((HALF, FEAT), BF),
            vmem((TOKENS, FEAT), BF),
            vmem((TOKENS, FEAT), BF),
            vmem((XS, TOKENS, FEAT), BF),
            vmem((TOKENS, FEAT), BF),
            vmem((TOKENS, FEAT), BF),
            vmem((TOKENS, FEAT), BF),
            vmem((ROWS, HEAD_DIM), BF),
            vmem((TOKENS, FEAT), F32),
            vmem((SLOTS, 1, TOKENS), F32),
            vmem((SLOTS, 1, TOKENS), F32),
            dma((8,)), dma((XS,)), dma((XS,)), dma((XS,)),
            dma((8, 2)), dma((SLOTS, 2)), dma, dma,
            dma((6,)), dma((6,)), dma((6,)), dma((6,)), dma, dma,
            dma((SLOTS,)), dma((SLOTS,)),
        ],
        compiler_params=pltpu.CompilerParams(
            collective_id=0, has_side_effects=True, vmem_limit_bytes=60 << 20
        ),
        name="relevance",
    )(queries, keys, values, w_out, relevance_out, segment_ids.reshape(CTX, TOKENS))


def solution(mesh):
    placed = (P("ctx", "tp"), P("ctx", "tp"), P("ctx", "tp"), P("tp", None), P("ctx", "tp"), P())
    return jax.shard_map(
        on_device,
        mesh=mesh,
        in_specs=placed,
        out_specs=(P("ctx", "tp"), P("ctx", "tp")),
        check_vma=False,
    )
```

time: 243 us -> 53.7 us (0.22)
  the two profiles are of different devices: /device:TPU:416 before, /device:TPU:1 now
where the time goes in v1:
time: 53.7 us; the launch traced here: 53.5 us
  Pallas kernels  49.8 us (93%)
  local copies, waits for them, and re-layouts  2.99 us (6%)
  between operations  0.64 us (1%)
    pallas_call x1, Pallas kernels, on_device(): pl.pallas_call(kernel, out_shape=(jax.ShapeDtypeStruct((TOKENS, GROUP * H...  49.8 us
    unnamed x1, local copies, waits for them, and re-layouts  1.57 us
    pallas_call x1, local copies, waits for them, and re-layouts, on_device(): pl.pallas_call(kernel, out_shape=(jax.ShapeDtypeStruct((TOKENS, GROUP * H...  1.42 us

profile of v1, /device:TPU:1, one launch (start us, length us, event | category | flops | bytes accessed | tf_op | source)
XLA Modules:
  0.0 53.5 jit_solution(10345443523989328838)
XLA Ops:
  0.6 49.8 %relevance.1 = (bf16[128,512]{1,0:T(8,128)(2,1)}, f32[128,1]{1,0:T(8,128)}) custom-call(bf16[128,512]{1,0:T(8,128)(2,1)} %q_hbm.1, bf16[128,128]{1,0:T(8,128)(2,1)} %k_hbm.1, bf16[128,128]{1,0:T(8,128)(2,1)} %v_hbm.1, bf16[512,4096]{1,0:T(8,128)(2,1)} %w_hbm.1, bf16[128,512]{1,0:T(8,128)(2,1)} %rel_hbm.1, s32[64,128]{1,0:T(8,128)} %bitcast.1), custom_call_target="tpu_custom_call" | custom-call | tf_op jit(solution)/shard_map/relevance/pallas_call | solution.py:409
  50.5 1.4 %copy.8 = f32[128,1]{0,1:T(1,128)} copy(f32[128,1]{1,0:T(8,128)} %get-tuple-element.3) | data formatting | bytes 1024 | tf_op jit(solution)/shard_map/relevance/pallas_call | solution.py:409
  51.9 1.6 %copy.10 = bf16[128,512]{1,0:T(8,128)(2,1)} copy(bf16[128,512]{1,0:T(8,128)(2,1)} %get-tuple-element.6) | data formatting | bytes 262144

commit v2 on v1

--- a/solution.py
+++ b/solution.py
@@ -45,7 +45,7 @@
     base = me - y
     y_right = base + lax.rem(y + 1, 4)
     y_left = base + lax.rem(y + 3, 4)
-    up = lax.rem(me + 4, CTX)
+    up = me + 4
     other = 1 - core
     partner = x * 2 + other
     x_right_i = lax.rem(x + 1, XS)
@@ -85,20 +85,49 @@
     greet(me, partner)
     greet(me, x_right)
     greet(me, x_left)
-    for d in range(1, SLOTS):
-        greet(lax.rem(me + d, CTX), tp)
-        greet(lax.rem(me + CTX - d, CTX), tp)
-    pl.semaphore_wait(barrier, 19)
+    greet(y_right, tp)
+    greet(y_left, tp)
+
+    @pl.when(me < CTX - 4)
+    def _():
+        greet(me + 4, tp)
+
+    @pl.when(me >= 4)
+    def _():
+        greet(me - 4, tp)
+
+    @pl.when(me < SLOTS - 1)
+    def _():
+        for d in range(1, SLOTS):
+            @pl.when(me < d)
+            def _():
+                kv[d] = jnp.zeros((2, TOKENS, HEAD_DIM), BF)
+
+    pl.semaphore_wait(
+        barrier, 5 + jnp.where(me < CTX - 4, 1, 0) + jnp.where(me >= 4, 1, 0)
+    )
 
     def kv_copy(number, half, src, dst, ctx):
-        return remote(
-            kv.at[src, half], kv.at[dst, half], kv_send.at[number, half], kv_recv.at[dst, half], ctx, tp
-        )
+        return (
+            remote(
+                kv.at[src, half], kv.at[dst, half], kv_send.at[number, half], kv_recv.at[dst, half], ctx, tp
+            ),
+            (ctx >= dst) & (ctx < CTX),
+        )
+
+    def start(pair):
+        copy, exists = pair
+
+        @pl.when(exists)
+        def _():
+            copy.start()
 
     def arrive(slot, half):
-        remote(
-            kv.at[slot, half], kv.at[slot, half], kv_send.at[0, half], kv_recv.at[slot, half], me, tp
-        ).wait_recv()
+        @pl.when(me >= slot)
+        def _():
+            remote(
+                kv.at[slot, half], kv.at[slot, half], kv_send.at[0, half], kv_recv.at[slot, half], me, tp
+            ).wait_recv()
 
     right_src = jnp.where(y < 3, 0, 8)
     right_dst = jnp.where(y < 3, 1, 5)
@@ -134,19 +163,19 @@
         return kv_copy(7, half, relay_left_src, 6, y_left)
 
     loads[0].wait()
-    up_one(0).start()
+    start(up_one(0))
     loads[1].wait()
-    up_one(1).start()
+    start(up_one(1))
 
     @pl.when(y < 3)
     def _():
-        right_zero(0).start()
-        right_zero(1).start()
+        start(right_zero(0))
+        start(right_zero(1))
 
     @pl.when(y == 0)
     def _():
-        left_zero(0).start()
-        left_zero(1).start()
+        start(left_zero(0))
+        start(left_zero(1))
 
     w_copies = []
     for i in range(XS):
@@ -191,9 +220,9 @@
 
     for half in range(2):
         arrive(4, half)
-        up_two(half).start()
-        right_one(half).start()
-        left_one(half).start()
+        start(up_two(half))
+        start(right_one(half))
+        start(left_one(half))
     score_block(4)
 
     inner_y = (y == 1) | (y == 2)
@@ -206,7 +235,7 @@
 
             @pl.when(y < 3)
             def _():
-                relay_right(half).start()
+                start(relay_right(half))
 
     @pl.when(y == 3)
     def _():
@@ -218,11 +247,11 @@
 
         @pl.when(y > 0)
         def _():
-            left_zero(half).start()
+            start(left_zero(half))
 
         @pl.when(y == 3)
         def _():
-            right_zero(half).start()
+            start(right_zero(half))
 
     score_block(jnp.where(y > 0, 1, 8))
 
@@ -233,13 +262,13 @@
 
         @pl.when(outer_y)
         def _():
-            relay_right(half).start()
+            start(relay_right(half))
 
         arrive(one_right, half)
 
         @pl.when(outer_y)
         def _():
-            relay_left(half).start()
+            start(relay_left(half))
 
     score_block(jnp.where(y > 0, 8, 1))
     score_block(5 - jnp.where(y > 0, 0, 2))
@@ -255,7 +284,7 @@
 
             @pl.when(inner_y)
             def _():
-                relay_left(half).start()
+                start(relay_left(half))
 
     score_block(jnp.where(y > 0, 3, 5))
     score_block(7)
@@ -375,24 +404,39 @@
     def term_copy(slot):
         return remote(
             term_out.at[slot], term_in.at[slot], t_send.at[slot], t_recv.at[slot],
-            lax.rem(me + CTX - slot, CTX), tp,
+            me - slot, tp,
         )
 
     for slot in range(SLOTS - 1, 0, -1):
         term_out[slot] = term(slot)
-        term_copy(slot).start()
+
+        @pl.when(me >= slot)
+        def _():
+            term_copy(slot).start()
+
+        @pl.when(me + slot >= CTX)
+        def _():
+            term_in[slot] = jnp.zeros((1, TOKENS), F32)
+
     own = term(0)
     for slot in range(1, SLOTS):
-        term_copy(slot).wait_recv()
+        @pl.when(me + slot < CTX)
+        def _():
+            term_copy(slot).wait_recv()
+
         own = own + term_in[slot]
-    tokens_ref[...] = jnp.broadcast_to(own, (TOKENS, TOKENS)).T[:, 0:1]
+    tokens_ref[...] = own
 
     heads_copy.wait()
     for copy in w_copies[1::2]:
         copy.wait_send()
     for half in range(2):
         for make in (up_one, up_two, right_zero, left_zero, right_one, left_one, relay_right, relay_left):
-            make(half).wait_send()
+            copy, exists = make(half)
+
+            @pl.when(exists)
+            def _():
+                copy.wait_send()
     a_copy.wait_send()
     for copy in (far_right, far_left, near_right, near_left, last_right, last_left):
         copy.wait_send()
@@ -400,17 +444,19 @@
         copy.wait_send()
     cross.wait_send()
     for slot in range(1, SLOTS):
-        term_copy(slot).wait_send()
+        @pl.when(me >= slot)
+        def _():
+            term_copy(slot).wait_send()
 
 
 def on_device(queries, keys, values, w_out, relevance_out, segment_ids):
     anywhere = pl.BlockSpec(memory_space=pl.ANY)
     vmem, dma = pltpu.VMEM, pltpu.SemaphoreType.DMA
-    return pl.pallas_call(
+    heads, tokens = pl.pallas_call(
         kernel,
         out_shape=(
             jax.ShapeDtypeStruct((TOKENS, GROUP * HEAD_DIM), BF),
-            jax.ShapeDtypeStruct((TOKENS, 1), F32),
+            jax.ShapeDtypeStruct((1, TOKENS), F32),
         ),
         in_specs=[anywhere] * 6,
         out_specs=(anywhere, pl.BlockSpec(memory_space=pltpu.VMEM)),
@@ -451,6 +497,7 @@
         ),
         name="relevance",
     )(queries, keys, values, w_out, relevance_out, segment_ids.reshape(CTX, TOKENS))
+    return heads, tokens.T
 
 
 def solution(mesh):

time: 53.7 us -> 46.4 us (0.86); the launches traced: 53.5 us -> 45.5 us
  Pallas kernels: 49.8 us -> 42.2 us
    pallas_call x1, Pallas kernels: 49.8 us -> 42.2 us  [on_device(): pl.pallas_call(kernel, out_shape=(jax.ShapeDtypeStruct((TOKENS, GROUP * H...]
    pallas_call x1 -> x0, local copies, waits for them, and re-layouts: 1.42 us -> none  [on_device(): pl.pallas_call(kernel, out_shape=(jax.ShapeDtypeStruct((TOKENS, GROUP * H...]
    unnamed x1 -> x2, local copies, waits for them, and re-layouts: 1.57 us -> 2.74 us
where the time goes in v2:
time: 46.4 us; the launch traced here: 45.5 us
  Pallas kernels  42.2 us (91%)
  local copies, waits for them, and re-layouts  2.74 us (6%)
  between operations  0.64 us (1%)
    pallas_call x1, Pallas kernels, on_device(): pl.pallas_call(kernel, out_shape=(jax.ShapeDtypeStruct((TOKENS, GROUP * H...  42.2 us
    unnamed x2, local copies, waits for them, and re-layouts  2.74 us

profile of v2, /device:TPU:1, one launch (start us, length us, event | category | flops | bytes accessed | tf_op | source)
XLA Modules:
  0.0 45.5 jit_solution(8748628561546065155)
XLA Ops:
  0.6 42.2 %relevance.1 = (bf16[128,512]{1,0:T(8,128)(2,1)}, f32[1,128]{1,0:T(1,128)}) custom-call(bf16[128,512]{1,0:T(8,128)(2,1)} %q_hbm.1, bf16[128,128]{1,0:T(8,128)(2,1)} %k_hbm.1, bf16[128,128]{1,0:T(8,128)(2,1)} %v_hbm.1, bf16[512,4096]{1,0:T(8,128)(2,1)} %w_hbm.1, bf16[128,512]{1,0:T(8,128)(2,1)} %rel_hbm.1, s32[64,128]{1,0:T(8,128)} %bitcast.2), custom_call_target="tpu_custom_call" | custom-call | tf_op jit(solution)/shard_map/relevance/pallas_call | solution.py:455
  42.8 1.6 %copy.10 = bf16[128,512]{1,0:T(8,128)(2,1)} copy(bf16[128,512]{1,0:T(8,128)(2,1)} %get-tuple-element.8) | data formatting | bytes 262144
  44.4 1.2 %copy.11 = f32[128,1]{0,1:T(1,128)} copy(f32[128,1]{0,1:T(1,128)} %bitcast.3) | data formatting | bytes 1024

commit v3 on v2

--- a/solution.py
+++ b/solution.py
@@ -14,7 +14,7 @@
 CTX = 64
 XS = 4
 FEAT = 512
-HALF = TOKENS // 2
+QUARTER = TOKENS // 4
 BF = jnp.bfloat16
 F32 = jnp.float32
 MASKED = -1e30
@@ -30,10 +30,9 @@
 
 
 def kernel(
-    q_hbm, k_hbm, v_hbm, w_hbm, rel_hbm, seg_hbm, heads_hbm, tokens_ref,
-    q, kv, w, rel, seg, score, weight, peak, att, send_two, from_far_left, from_far_right,
-    merged_right, merged_left, direct_right, direct_left, in_left, in_right,
-    ratio, cross_out, cross_in, heads, passed, inverse, term_out, term_in,
+    q_hbm, k_hbm, v_hbm, w_hbm, rel_hbm, seg_hbm, heads, tokens_ref,
+    q, kv, w, rel, seg, score, weight, peak, att, far_out, far_in, right_out, left_out, left_in, right_in, near,
+    ratio, cross_out, cross_in, values_flipped, passed, inverse, term_out, term_in,
     local_sem, w_local_sem, w_send, w_recv, kv_send, kv_recv, a_send, a_recv,
     rs_send, rs_recv, ag_send, ag_recv, c_send, c_recv, t_send, t_recv,
 ):
@@ -215,6 +214,7 @@
                 peak[rows, :] = s
             else:
                 peak[rows, :] = jnp.maximum(peak[rows, :], s)
+        values_flipped[slot] = kv[slot, 1].T
 
     score_block(0, True)
 
@@ -323,65 +323,83 @@
     def project(i):
         return dot_nn(att[core], w[core, i]) + dot_nn(att[other], w[other, i])
 
-    def rs(number, src, dst, tpi):
-        return remote(src, dst, rs_send.at[number], rs_recv.at[number], me, tpi)
-
-    send_two[...] = project(x_far_i).astype(BF)
-    top_rows, low_rows = pl.ds(0, HALF), pl.ds(HALF, HALF)
-    far_right = rs(0, send_two.at[top_rows], from_far_left, x_right)
-    far_left = rs(1, send_two.at[low_rows], from_far_right, x_left)
-    far_right.start()
-    far_left.start()
-    to_right = project(x_right_i)
-    direct_right[...] = to_right[HALF:].astype(BF)
-    near_right = rs(2, direct_right, in_left.at[low_rows], x_right)
-    near_right.start()
-    to_left = project(x_left_i)
-    direct_left[...] = to_left[:HALF].astype(BF)
-    near_left = rs(3, direct_left, in_right.at[top_rows], x_left)
-    near_left.start()
-    far_right.wait_recv()
-    merged_right[...] = (to_right[:HALF] + from_far_left[...].astype(F32)).astype(BF)
-    last_right = rs(4, merged_right, in_left.at[top_rows], x_right)
-    last_right.start()
-    far_left.wait_recv()
-    merged_left[...] = (to_left[HALF:] + from_far_right[...].astype(F32)).astype(BF)
-    last_left = rs(5, merged_left, in_right.at[low_rows], x_left)
-    last_left.start()
-    mine = project(x)
-    for copy in (near_right, near_left, last_right, last_left):
-        copy.wait_recv()
-
-    total = mine + in_left[...].astype(F32) + in_right[...].astype(F32)
-    ratio[x] = (rel[...].astype(F32) * total / (total * total + 1.0)).astype(BF)
-
-    def ag(number, owner, rows, tpi):
+    quarter = [pl.ds(i * QUARTER, QUARTER) for i in range(4)]
+
+    def rs(kind, i, src, dst, tpi):
+        return remote(src, dst, rs_send.at[kind, i], rs_recv.at[kind, i], me, tpi)
+
+    def rs_far(i):
+        return rs(0, i, far_out.at[quarter[i]], far_in.at[quarter[i]], x_left if i % 2 else x_right)
+
+    def rs_near(i):
+        if i % 2:
+            return rs(1, i, right_out.at[quarter[i]], left_in.at[quarter[i]], x_right)
+        return rs(1, i, left_out.at[quarter[i]], right_in.at[quarter[i]], x_left)
+
+    def rs_merged(i):
+        if i % 2:
+            return rs(2, i, left_out.at[quarter[i]], right_in.at[quarter[i]], x_left)
+        return rs(2, i, right_out.at[quarter[i]], left_in.at[quarter[i]], x_right)
+
+    far_out[...] = project(x_far_i).astype(BF)
+    for i in range(4):
+        rs_far(i).start()
+    near[0] = project(x_right_i)
+    for i in (1, 3):
+        right_out[quarter[i], :] = near[0, quarter[i], :].astype(BF)
+        rs_near(i).start()
+    near[1] = project(x_left_i)
+    for i in (0, 2):
+        left_out[quarter[i], :] = near[1, quarter[i], :].astype(BF)
+        rs_near(i).start()
+    near[2] = project(x)
+    for i in range(4):
+        rs_far(i).wait_recv()
+        merged = (near[i % 2, quarter[i], :] + far_in[quarter[i], :].astype(F32)).astype(BF)
+        if i % 2:
+            left_out[quarter[i], :] = merged
+        else:
+            right_out[quarter[i], :] = merged
+        rs_merged(i).start()
+
+    def ag(kind, i, owner, tpi):
         return remote(
-            ratio.at[owner, rows], ratio.at[owner, rows], ag_send.at[number], ag_recv.at[number], me, tpi
-        )
-
-    shares = [
-        ag(0, x, top_rows, x_right), ag(1, x, low_rows, x_left),
-        ag(2, x, low_rows, x_right), ag(3, x, top_rows, x_left),
-    ]
-    for copy in shares:
-        copy.start()
+            ratio.at[owner, quarter[i]], ratio.at[owner, quarter[i]],
+            ag_send.at[kind, i], ag_recv.at[kind, i], me, tpi,
+        )
+
+    def ag_first(i, owner):
+        return ag(0, i, owner, x_left if i % 2 else x_right)
+
+    def ag_second(i, owner):
+        return ag(1, i, owner, x_right if i % 2 else x_left)
+
+    def ag_relay(i, owner):
+        return ag(2, i, owner, x_left if i % 2 else x_right)
+
+    for half in range(2):
+        for i in (2 * half, 2 * half + 1):
+            rs_near(i).wait_recv()
+            rs_merged(i).wait_recv()
+            rows = quarter[i]
+            total = near[2, rows, :] + left_in[rows, :].astype(F32) + right_in[rows, :].astype(F32)
+            ratio[x, rows, :] = (rel[rows, :].astype(F32) * total / (total * total + 1.0)).astype(BF)
+            ag_first(i, x).start()
+    for i in range(4):
+        ag_second(i, x).start()
     back_other = dot_nt(ratio[x], w[other, x])
     back_own = dot_nt(ratio[x], w[core, x])
-    ag(0, x_left_i, top_rows, x_right).wait_recv()
-    pass_right = ag(4, x_left_i, top_rows, x_right)
-    pass_right.start()
-    ag(1, x_right_i, low_rows, x_left).wait_recv()
-    pass_left = ag(5, x_right_i, low_rows, x_left)
-    pass_left.start()
-    ag(2, x_left_i, low_rows, x_right).wait_recv()
-    back_other += dot_nt(ratio[x_left_i], w[other, x_left_i])
-    back_own += dot_nt(ratio[x_left_i], w[core, x_left_i])
-    ag(3, x_right_i, top_rows, x_left).wait_recv()
-    back_other += dot_nt(ratio[x_right_i], w[other, x_right_i])
-    back_own += dot_nt(ratio[x_right_i], w[core, x_right_i])
-    ag(4, x_far_i, top_rows, x_right).wait_recv()
-    ag(5, x_far_i, low_rows, x_left).wait_recv()
+    for i in range(4):
+        owner = x_right_i if i % 2 else x_left_i
+        ag_first(i, owner).wait_recv()
+        ag_relay(i, owner).start()
+    for i in range(4):
+        ag_second(i, x_left_i if i % 2 else x_right_i).wait_recv()
+    for owner in (x_left_i, x_right_i):
+        back_other += dot_nt(ratio[owner], w[other, owner])
+        back_own += dot_nt(ratio[owner], w[core, owner])
+    for i in range(4):
+        ag_relay(i, x_far_i).wait_recv()
     back_other += dot_nt(ratio[x_far_i], w[other, x_far_i])
     cross_out[...] = back_other.astype(BF)
     cross = remote(cross_out, cross_in, c_send, c_recv, me, partner)
@@ -391,15 +409,16 @@
     a = att[core].astype(F32)
     carried = a * (back_own + cross_in[...].astype(F32))
     heads[...] = carried.astype(BF)
-    heads_copy = pltpu.make_async_copy(heads, heads_hbm, local_sem.at[0])
-    heads_copy.start()
     scaled = carried * a / (a * a + 1.0) * inverse[...]
     for h in range(GROUP):
         passed[h * TOKENS:(h + 1) * TOKENS, :] = scaled[:, h * HEAD_DIM:(h + 1) * HEAD_DIM].astype(BF)
 
     def term(slot):
-        inner = dot_nt(passed[...], kv[slot, 1])
-        return jnp.sum(score[slot] * inner, axis=0, keepdims=True)
+        total = jnp.zeros((TOKENS, TOKENS), F32)
+        for h in range(GROUP):
+            rows = pl.ds(h * TOKENS, TOKENS)
+            total = total + score[slot, rows, :] * dot_nn(passed[rows, :], values_flipped[slot])
+        return jnp.sum(total, axis=0, keepdims=True)
 
     def term_copy(slot):
         return remote(
@@ -427,7 +446,6 @@
         own = own + term_in[slot]
     tokens_ref[...] = own
 
-    heads_copy.wait()
     for copy in w_copies[1::2]:
         copy.wait_send()
     for half in range(2):
@@ -438,15 +456,28 @@
             def _():
                 copy.wait_send()
     a_copy.wait_send()
-    for copy in (far_right, far_left, near_right, near_left, last_right, last_left):
-        copy.wait_send()
-    for copy in shares + [pass_right, pass_left]:
-        copy.wait_send()
+    for i in range(4):
+        owner = x_right_i if i % 2 else x_left_i
+        for copy in (
+            rs_far(i), rs_near(i), rs_merged(i), ag_first(i, x), ag_second(i, x), ag_relay(i, owner)
+        ):
+            copy.wait_send()
     cross.wait_send()
     for slot in range(1, SLOTS):
         @pl.when(me >= slot)
         def _():
             term_copy(slot).wait_send()
+
+
+def leave(heads, tokens, heads_out, tokens_out, sem):
+    copies = [
+        pltpu.make_async_copy(heads, heads_out, sem.at[0]),
+        pltpu.make_async_copy(tokens, tokens_out, sem.at[1]),
+    ]
+    for copy in copies:
+        copy.start()
+    for copy in copies:
+        copy.wait()
 
 
 def on_device(queries, keys, values, w_out, relevance_out, segment_ids):
@@ -455,11 +486,11 @@
     heads, tokens = pl.pallas_call(
         kernel,
         out_shape=(
-            jax.ShapeDtypeStruct((TOKENS, GROUP * HEAD_DIM), BF),
-            jax.ShapeDtypeStruct((1, TOKENS), F32),
+            pltpu.VMEM((TOKENS, GROUP * HEAD_DIM), BF),
+            pltpu.VMEM((1, TOKENS), F32),
         ),
         in_specs=[anywhere] * 6,
-        out_specs=(anywhere, pl.BlockSpec(memory_space=pltpu.VMEM)),
+        out_specs=(pl.BlockSpec(memory_space=pltpu.VMEM), pl.BlockSpec(memory_space=pltpu.VMEM)),
         scratch_shapes=[
             vmem((ROWS, HEAD_DIM), BF),
             vmem((SLOTS, 2, TOKENS, HEAD_DIM), BF),
@@ -471,25 +502,23 @@
             vmem((ROWS, TOKENS), F32),
             vmem((2, TOKENS, FEAT), BF),
             vmem((TOKENS, FEAT), BF),
-            vmem((HALF, FEAT), BF),
-            vmem((HALF, FEAT), BF),
-            vmem((HALF, FEAT), BF),
-            vmem((HALF, FEAT), BF),
-            vmem((HALF, FEAT), BF),
-            vmem((HALF, FEAT), BF),
-            vmem((TOKENS, FEAT), BF),
-            vmem((TOKENS, FEAT), BF),
+            vmem((TOKENS, FEAT), BF),
+            vmem((TOKENS, FEAT), BF),
+            vmem((TOKENS, FEAT), BF),
+            vmem((TOKENS, FEAT), BF),
+            vmem((TOKENS, FEAT), BF),
+            vmem((3, TOKENS, FEAT), F32),
             vmem((XS, TOKENS, FEAT), BF),
             vmem((TOKENS, FEAT), BF),
             vmem((TOKENS, FEAT), BF),
-            vmem((TOKENS, FEAT), BF),
+            vmem((SLOTS, HEAD_DIM, TOKENS), BF),
             vmem((ROWS, HEAD_DIM), BF),
             vmem((TOKENS, FEAT), F32),
             vmem((SLOTS, 1, TOKENS), F32),
             vmem((SLOTS, 1, TOKENS), F32),
             dma((8,)), dma((XS,)), dma((XS,)), dma((XS,)),
             dma((8, 2)), dma((SLOTS, 2)), dma, dma,
-            dma((6,)), dma((6,)), dma((6,)), dma((6,)), dma, dma,
+            dma((3, 4)), dma((3, 4)), dma((3, 4)), dma((3, 4)), dma, dma,
             dma((SLOTS,)), dma((SLOTS,)),
         ],
         compiler_params=pltpu.CompilerParams(
@@ -497,6 +526,17 @@
         ),
         name="relevance",
     )(queries, keys, values, w_out, relevance_out, segment_ids.reshape(CTX, TOKENS))
+    heads, tokens = pl.pallas_call(
+        leave,
+        out_shape=(
+            jax.ShapeDtypeStruct((TOKENS, GROUP * HEAD_DIM), BF),
+            jax.ShapeDtypeStruct((1, TOKENS), F32),
+        ),
+        in_specs=[pl.BlockSpec(memory_space=pltpu.VMEM)] * 2,
+        out_specs=(anywhere, anywhere),
+        scratch_shapes=[dma((2,))],
+        name="leave",
+    )(*[pltpu.with_memory_space_constraint(a, pltpu.VMEM) for a in (heads, tokens)])
     return heads, tokens.T
 
 

time: 46.4 us -> 42.4 us (0.914)
  the two profiles are of different devices: /device:TPU:1 before, /device:TPU:248 now
where the time goes in v3:
time: 42.4 us; the launch traced here: 42.3 us
  Pallas kernels  41.7 us (98%)
  between operations  0.64 us (2%)
    pallas_call x1, Pallas kernels, on_device(): pl.pallas_call(kernel, out_shape=(pltpu.VMEM((TOKENS, GROUP * HEAD_DIM),...  41 us

profile of v3, /device:TPU:248, one launch (start us, length us, event | category | flops | bytes accessed | tf_op | source)
XLA Modules:
  0.0 42.3 jit_solution(9278096393169529558)
XLA Ops:
  0.6 41.0 %relevance.1 = (bf16[128,512]{1,0:T(8,128)(2,1)S(1)}, f32[1,128]{1,0:T(1,128)S(1)}) custom-call(bf16[128,512]{1,0:T(8,128)(2,1)} %q_hbm.1, bf16[128,128]{1,0:T(8,128)(2,1)} %k_hbm.1, bf16[128,128]{1,0:T(8,128)(2,1)} %v_hbm.1, bf16[512,4096]{1,0:T(8,128)(2,1)} %w_hbm.1, bf16[128,512]{1,0:T(8,128)(2,1)} %rel_hbm.1, s32[64,128]{1,0:T(8,128)} %bitcast.2), custom_call_target="tpu_custom_call" | custom-call | tf_op jit(solution)/shard_map/relevance/pallas_call | solution.py:486
  41.6 0.7 %leave.1 = (bf16[128,512]{1,0:T(8,128)(2,1)}, f32[1,128]{1,0:T(1,128)}) custom-call(bf16[128,512]{1,0:T(8,128)(2,1)S(1)} %get-tuple-element.6.heads, f32[1,128]{1,0:T(1,128)S(1)} %get-tuple-element.7.tokens), custom_call_target="tpu_custom_call" | custom-call | tf_op jit(solution)/shard_map/leave/pallas_call | solution.py:529

commit v4 on v3

--- a/solution.py
+++ b/solution.py
@@ -63,16 +63,16 @@
         pltpu.make_async_copy(k_hbm, kv.at[0, 0], local_sem.at[0]),
         pltpu.make_async_copy(v_hbm, kv.at[0, 1], local_sem.at[1]),
         pltpu.make_async_copy(seg_hbm, seg, local_sem.at[2]),
+        pltpu.make_async_copy(rel_hbm, rel, local_sem.at[3]),
     ]
     for h in range(GROUP):
         loads.append(
             pltpu.make_async_copy(
                 q_hbm.at[:, h * HEAD_DIM:(h + 1) * HEAD_DIM],
                 q.at[h * TOKENS:(h + 1) * TOKENS, :],
-                local_sem.at[3 + h],
+                local_sem.at[4],
             )
         )
-    loads.append(pltpu.make_async_copy(rel_hbm, rel, local_sem.at[7]))
     for load in loads:
         load.start()
 
@@ -84,6 +84,7 @@
     greet(me, partner)
     greet(me, x_right)
     greet(me, x_left)
+    greet(base + lax.rem(y + 2, 4), tp)
     greet(y_right, tp)
     greet(y_left, tp)
 
@@ -103,13 +104,13 @@
                 kv[d] = jnp.zeros((2, TOKENS, HEAD_DIM), BF)
 
     pl.semaphore_wait(
-        barrier, 5 + jnp.where(me < CTX - 4, 1, 0) + jnp.where(me >= 4, 1, 0)
+        barrier, 6 + jnp.where(me < CTX - 4, 1, 0) + jnp.where(me >= 4, 1, 0)
     )
 
     def kv_copy(number, half, src, dst, ctx):
         return (
             remote(
-                kv.at[src, half], kv.at[dst, half], kv_send.at[number, half], kv_recv.at[dst, half], ctx, tp
+                kv.at[src, half], kv.at[dst, half], kv_send.at[number], kv_recv.at[dst, half], ctx, tp
             ),
             (ctx >= dst) & (ctx < CTX),
         )
@@ -125,9 +126,10 @@
         @pl.when(me >= slot)
         def _():
             remote(
-                kv.at[slot, half], kv.at[slot, half], kv_send.at[0, half], kv_recv.at[slot, half], me, tp
+                kv.at[slot, half], kv.at[slot, half], kv_send.at[0], kv_recv.at[slot, half], me, tp
             ).wait_recv()
 
+    outer_y = (y == 0) | (y == 3)
     right_src = jnp.where(y < 3, 0, 8)
     right_dst = jnp.where(y < 3, 1, 5)
     left_src = jnp.where(y > 0, 8, 0)
@@ -159,7 +161,12 @@
         return kv_copy(6, half, relay_right_src, 2, y_right)
 
     def relay_left(half):
-        return kv_copy(7, half, relay_left_src, 6, y_left)
+        copy, exists = kv_copy(7, half, relay_left_src, 6, y_left)
+        return copy, exists & outer_y
+
+    def far_back(half):
+        copy, exists = kv_copy(8, half, 8, 6, me - 2)
+        return copy, exists & (y >= 2)
 
     loads[0].wait()
     start(up_one(0))
@@ -181,20 +188,21 @@
         w_copies.append(
             pltpu.make_async_copy(
                 w_hbm.at[:, pl.ds(pl.multiple_of((2 * i + core) * FEAT, FEAT), FEAT)],
-                w.at[core, i], w_local_sem.at[i],
+                w.at[core, i], w_local_sem,
             )
         )
         w_copies.append(
             remote(
                 w_hbm.at[:, pl.ds(pl.multiple_of((2 * i + other) * FEAT, FEAT), FEAT)],
-                w.at[core, i], w_send.at[i], w_recv.at[i], me, partner,
+                w.at[core, i], w_send, w_recv, me, partner,
             )
         )
     for copy in w_copies:
         copy.start()
 
-    for load in loads[2:]:
+    for load in loads[2:4]:
         load.wait()
+    pltpu.make_async_copy(q, q, local_sem.at[4]).wait()
 
     own_seg = jnp.broadcast_to(seg[pl.ds(me, 1), :].astype(F32), (TOKENS, TOKENS)).T
     row_at = lax.broadcasted_iota(jnp.int32, (TOKENS, TOKENS), 0)
@@ -225,8 +233,6 @@
         start(left_one(half))
     score_block(4)
 
-    inner_y = (y == 1) | (y == 2)
-    outer_y = (y == 0) | (y == 3)
 
     @pl.when(y > 0)
     def _():
@@ -252,6 +258,8 @@
         @pl.when(y == 3)
         def _():
             start(right_zero(half))
+
+        start(far_back(half))
 
     score_block(jnp.where(y > 0, 1, 8))
 
@@ -266,9 +274,7 @@
 
         arrive(one_right, half)
 
-        @pl.when(outer_y)
-        def _():
-            start(relay_left(half))
+        start(relay_left(half))
 
     score_block(jnp.where(y > 0, 8, 1))
     score_block(5 - jnp.where(y > 0, 0, 2))
@@ -281,10 +287,6 @@
     def _():
         for half in range(2):
             arrive(7, half)
-
-            @pl.when(inner_y)
-            def _():
-                start(relay_left(half))
 
     score_block(jnp.where(y > 0, 3, 5))
     score_block(7)
@@ -314,10 +316,8 @@
 
     a_copy = remote(att.at[core], att.at[core], a_send, a_recv, me, partner)
     a_copy.start()
-    for copy in w_copies[0::2]:
-        copy.wait()
-    for copy in w_copies[1::2]:
-        copy.wait_recv()
+    pltpu.make_async_copy(w.at[core], w.at[core], w_local_sem).wait()
+    remote(w.at[core], w.at[other], w_send, w_recv, me, partner).wait_recv()
     remote(att.at[other], att.at[other], a_send, a_recv, me, partner).wait_recv()
 
     def project(i):
@@ -326,7 +326,7 @@
     quarter = [pl.ds(i * QUARTER, QUARTER) for i in range(4)]
 
     def rs(kind, i, src, dst, tpi):
-        return remote(src, dst, rs_send.at[kind, i], rs_recv.at[kind, i], me, tpi)
+        return remote(src, dst, rs_send, rs_recv.at[4 + i // 2 if kind else i], me, tpi)
 
     def rs_far(i):
         return rs(0, i, far_out.at[quarter[i]], far_in.at[quarter[i]], x_left if i % 2 else x_right)
@@ -365,7 +365,7 @@
     def ag(kind, i, owner, tpi):
         return remote(
             ratio.at[owner, quarter[i]], ratio.at[owner, quarter[i]],
-            ag_send.at[kind, i], ag_recv.at[kind, i], me, tpi,
+            ag_send, ag_recv.at[3 + kind if kind else i], me, tpi,
         )
 
     def ag_first(i, owner):
@@ -378,9 +378,8 @@
         return ag(2, i, owner, x_left if i % 2 else x_right)
 
     for half in range(2):
+        remote(left_in, left_in, rs_send, rs_recv.at[4 + half], me, x_left).wait_recv()
         for i in (2 * half, 2 * half + 1):
-            rs_near(i).wait_recv()
-            rs_merged(i).wait_recv()
             rows = quarter[i]
             total = near[2, rows, :] + left_in[rows, :].astype(F32) + right_in[rows, :].astype(F32)
             ratio[x, rows, :] = (rel[rows, :].astype(F32) * total / (total * total + 1.0)).astype(BF)
@@ -393,13 +392,11 @@
         owner = x_right_i if i % 2 else x_left_i
         ag_first(i, owner).wait_recv()
         ag_relay(i, owner).start()
-    for i in range(4):
-        ag_second(i, x_left_i if i % 2 else x_right_i).wait_recv()
+    remote(ratio.at[x], ratio.at[x_left_i], ag_send, ag_recv.at[4], me, x_left).wait_recv()
     for owner in (x_left_i, x_right_i):
         back_other += dot_nt(ratio[owner], w[other, owner])
         back_own += dot_nt(ratio[owner], w[core, owner])
-    for i in range(4):
-        ag_relay(i, x_far_i).wait_recv()
+    remote(ratio.at[x], ratio.at[x_far_i], ag_send, ag_recv.at[5], me, x_left).wait_recv()
     back_other += dot_nt(ratio[x_far_i], w[other, x_far_i])
     cross_out[...] = back_other.astype(BF)
     cross = remote(cross_out, cross_in, c_send, c_recv, me, partner)
@@ -422,13 +419,13 @@
 
     def term_copy(slot):
         return remote(
-            term_out.at[slot], term_in.at[slot], t_send.at[slot], t_recv.at[slot],
+            term_out.at[slot], term_in.at[slot], t_send, t_recv,
             me - slot, tp,
         )
 
     for slot in range(SLOTS - 1, 0, -1):
         term_out[slot] = term(slot)
-
+    for slot in range(SLOTS - 1, 0, -1):
         @pl.when(me >= slot)
         def _():
             term_copy(slot).start()
@@ -438,35 +435,36 @@
             term_in[slot] = jnp.zeros((1, TOKENS), F32)
 
     own = term(0)
+    for count in range(1, SLOTS):
+        @pl.when(jnp.minimum(SLOTS - 1, CTX - 1 - me) == count)
+        def _():
+            some = pl.ds(1, count)
+            remote(term_out.at[some], term_in.at[some], t_send, t_recv, me, tp).wait_recv()
+
     for slot in range(1, SLOTS):
-        @pl.when(me + slot < CTX)
-        def _():
-            term_copy(slot).wait_recv()
-
         own = own + term_in[slot]
     tokens_ref[...] = own
 
-    for copy in w_copies[1::2]:
-        copy.wait_send()
-    for half in range(2):
-        for make in (up_one, up_two, right_zero, left_zero, right_one, left_one, relay_right, relay_left):
-            copy, exists = make(half)
-
-            @pl.when(exists)
-            def _():
-                copy.wait_send()
+    remote(w.at[core], w.at[other], w_send, w_recv, me, partner).wait_send()
+    for number, make in enumerate(
+        (up_one, up_two, right_zero, left_zero, right_one, left_one, relay_right, relay_left, far_back)
+    ):
+        exists = make(0)[1]
+
+        @pl.when(exists)
+        def _():
+            remote(kv.at[0], kv.at[0], kv_send.at[number], kv_recv.at[0, 0], me, tp).wait_send()
+
     a_copy.wait_send()
-    for i in range(4):
-        owner = x_right_i if i % 2 else x_left_i
-        for copy in (
-            rs_far(i), rs_near(i), rs_merged(i), ag_first(i, x), ag_second(i, x), ag_relay(i, owner)
-        ):
-            copy.wait_send()
+    twelve = w.at[0, 0, pl.ds(0, 3 * TOKENS)]
+    remote(twelve, twelve, rs_send, rs_recv.at[0], me, x_left).wait_send()
+    remote(twelve, twelve, ag_send, ag_recv.at[0], me, x_left).wait_send()
     cross.wait_send()
-    for slot in range(1, SLOTS):
-        @pl.when(me >= slot)
-        def _():
-            term_copy(slot).wait_send()
+    for count in range(1, SLOTS):
+        @pl.when(jnp.minimum(SLOTS - 1, me) == count)
+        def _():
+            some = pl.ds(1, count)
+            remote(term_out.at[some], term_in.at[some], t_send, t_recv, me, tp).wait_send()
 
 
 def leave(heads, tokens, heads_out, tokens_out, sem):
@@ -516,10 +514,10 @@
             vmem((TOKENS, FEAT), F32),
             vmem((SLOTS, 1, TOKENS), F32),
             vmem((SLOTS, 1, TOKENS), F32),
-            dma((8,)), dma((XS,)), dma((XS,)), dma((XS,)),
-            dma((8, 2)), dma((SLOTS, 2)), dma, dma,
-            dma((3, 4)), dma((3, 4)), dma((3, 4)), dma((3, 4)), dma, dma,
-            dma((SLOTS,)), dma((SLOTS,)),
+            dma((5,)), dma, dma, dma,
+            dma((9,)), dma((SLOTS, 2)), dma, dma,
+            dma, dma((6,)), dma, dma((6,)), dma, dma,
+            dma, dma,
         ],
         compiler_params=pltpu.CompilerParams(
             collective_id=0, has_side_effects=True, vmem_limit_bytes=60 << 20

time: 42.4 us -> 42.1 us (level)
  the two profiles are of different devices: /device:TPU:248 before, /device:TPU:1 now
where the time goes in v4:
time: 42.1 us; the launch traced here: 41.4 us
  Pallas kernels  40.8 us (97%)
  between operations  0.64 us (2%)
    pallas_call x1, Pallas kernels, on_device(): pl.pallas_call(kernel, out_shape=(pltpu.VMEM((TOKENS, GROUP * HEAD_DIM),...  40.1 us

profile of v4, /device:TPU:1, one launch (start us, length us, event | category | flops | bytes accessed | tf_op | source)
XLA Modules:
  0.0 41.4 jit_solution(4762343955074986819)
XLA Ops:
  0.6 40.1 %relevance.1 = (bf16[128,512]{1,0:T(8,128)(2,1)S(1)}, f32[1,128]{1,0:T(1,128)S(1)}) custom-call(bf16[128,512]{1,0:T(8,128)(2,1)} %q_hbm.1, bf16[128,128]{1,0:T(8,128)(2,1)} %k_hbm.1, bf16[128,128]{1,0:T(8,128)(2,1)} %v_hbm.1, bf16[512,4096]{1,0:T(8,128)(2,1)} %w_hbm.1, bf16[128,512]{1,0:T(8,128)(2,1)} %rel_hbm.1, s32[64,128]{1,0:T(8,128)} %bitcast.2), custom_call_target="tpu_custom_call" | custom-call | tf_op jit(solution)/shard_map/relevance/pallas_call | solution.py:484
  40.8 0.7 %leave.1 = (bf16[128,512]{1,0:T(8,128)(2,1)}, f32[1,128]{1,0:T(1,128)}) custom-call(bf16[128,512]{1,0:T(8,128)(2,1)S(1)} %get-tuple-element.6.heads, f32[1,128]{1,0:T(1,128)S(1)} %get-tuple-element.7.tokens), custom_call_target="tpu_custom_call" | custom-call | tf_op jit(solution)/shard_map/leave/pallas_call | solution.py:527

commit v5 on v4

--- a/solution.py
+++ b/solution.py
@@ -32,7 +32,7 @@
 def kernel(
     q_hbm, k_hbm, v_hbm, w_hbm, rel_hbm, seg_hbm, heads, tokens_ref,
     q, kv, w, rel, seg, score, weight, peak, att, far_out, far_in, right_out, left_out, left_in, right_in, near,
-    ratio, cross_out, cross_in, values_flipped, passed, inverse, term_out, term_in,
+    ratio, cross_out, cross_in, values_flipped, flipped, back, passed, inverse, term_out, term_in,
     local_sem, w_local_sem, w_send, w_recv, kv_send, kv_recv, a_send, a_recv,
     rs_send, rs_recv, ag_send, ag_recv, c_send, c_recv, t_send, t_recv,
 ):
@@ -129,7 +129,6 @@
                 kv.at[slot, half], kv.at[slot, half], kv_send.at[0], kv_recv.at[slot, half], me, tp
             ).wait_recv()
 
-    outer_y = (y == 0) | (y == 3)
     right_src = jnp.where(y < 3, 0, 8)
     right_dst = jnp.where(y < 3, 1, 5)
     left_src = jnp.where(y > 0, 8, 0)
@@ -137,7 +136,6 @@
     next_right_dst = jnp.where(y < 3, 5, 1)
     next_left_dst = jnp.where(y > 0, 3, 7)
     relay_right_src = jnp.where(y < 3, 1, 5)
-    relay_left_src = jnp.where(y > 0, 7, 3)
 
     def up_one(half):
         return kv_copy(0, half, 0, 4, up)
@@ -158,11 +156,11 @@
         return kv_copy(5, half, 4, next_left_dst, y_left)
 
     def relay_right(half):
-        return kv_copy(6, half, relay_right_src, 2, y_right)
-
-    def relay_left(half):
-        copy, exists = kv_copy(7, half, relay_left_src, 6, y_left)
-        return copy, exists & outer_y
+        copy, exists = kv_copy(6, half, relay_right_src, 2, y_right)
+        return copy, exists & ((y == 1) | (y == 2))
+
+    def below_two(half):
+        return kv_copy(7, half, 4, jnp.where(y < 2, 6, 2), jnp.where(y < 2, me + 2, me - 2))
 
     def far_back(half):
         copy, exists = kv_copy(8, half, 8, 6, me - 2)
@@ -222,13 +220,13 @@
                 peak[rows, :] = s
             else:
                 peak[rows, :] = jnp.maximum(peak[rows, :], s)
-        values_flipped[slot] = kv[slot, 1].T
 
     score_block(0, True)
 
     for half in range(2):
         arrive(4, half)
         start(up_two(half))
+        start(below_two(half))
         start(right_one(half))
         start(left_one(half))
     score_block(4)
@@ -267,14 +265,7 @@
     one_right = jnp.where(y < 3, 3, 7)
     for half in range(2):
         arrive(one_left, half)
-
-        @pl.when(outer_y)
-        def _():
-            start(relay_right(half))
-
         arrive(one_right, half)
-
-        start(relay_left(half))
 
     score_block(jnp.where(y > 0, 8, 1))
     score_block(5 - jnp.where(y > 0, 0, 2))
@@ -345,14 +336,19 @@
     for i in range(4):
         rs_far(i).start()
     near[0] = project(x_right_i)
-    for i in (1, 3):
-        right_out[quarter[i], :] = near[0, quarter[i], :].astype(BF)
+    near[1] = project(x_left_i)
+    near[2] = project(x)
+    for i in range(4):
+        if i % 2:
+            right_out[quarter[i], :] = near[0, quarter[i], :].astype(BF)
+        else:
+            left_out[quarter[i], :] = near[1, quarter[i], :].astype(BF)
+    for i in range(4):
         rs_near(i).start()
-    near[1] = project(x_left_i)
-    for i in (0, 2):
-        left_out[quarter[i], :] = near[1, quarter[i], :].astype(BF)
-        rs_near(i).start()
-    near[2] = project(x)
+    for slot in range(SLOTS):
+        values_flipped[slot] = kv[slot, 1].T
+    for j in range(2):
+        flipped[j] = w[j, x_far_i].T
     for i in range(4):
         rs_far(i).wait_recv()
         merged = (near[i % 2, quarter[i], :] + far_in[quarter[i], :].astype(F32)).astype(BF)
@@ -384,24 +380,24 @@
             total = near[2, rows, :] + left_in[rows, :].astype(F32) + right_in[rows, :].astype(F32)
             ratio[x, rows, :] = (rel[rows, :].astype(F32) * total / (total * total + 1.0)).astype(BF)
             ag_first(i, x).start()
+    back[0] = dot_nt(ratio[x], w[other, x])
+    back[1] = dot_nt(ratio[x], w[core, x])
     for i in range(4):
         ag_second(i, x).start()
-    back_other = dot_nt(ratio[x], w[other, x])
-    back_own = dot_nt(ratio[x], w[core, x])
     for i in range(4):
         owner = x_right_i if i % 2 else x_left_i
         ag_first(i, owner).wait_recv()
         ag_relay(i, owner).start()
     remote(ratio.at[x], ratio.at[x_left_i], ag_send, ag_recv.at[4], me, x_left).wait_recv()
     for owner in (x_left_i, x_right_i):
-        back_other += dot_nt(ratio[owner], w[other, owner])
-        back_own += dot_nt(ratio[owner], w[core, owner])
+        back[0] += dot_nt(ratio[owner], w[other, owner])
+        back[1] += dot_nt(ratio[owner], w[core, owner])
     remote(ratio.at[x], ratio.at[x_far_i], ag_send, ag_recv.at[5], me, x_left).wait_recv()
-    back_other += dot_nt(ratio[x_far_i], w[other, x_far_i])
+    back_other = back[0] + dot_nn(ratio[x_far_i], flipped[other])
     cross_out[...] = back_other.astype(BF)
     cross = remote(cross_out, cross_in, c_send, c_recv, me, partner)
     cross.start()
-    back_own += dot_nt(ratio[x_far_i], w[core, x_far_i])
+    back_own = back[1] + dot_nn(ratio[x_far_i], flipped[core])
     cross.wait_recv()
     a = att[core].astype(F32)
     carried = a * (back_own + cross_in[...].astype(F32))
@@ -447,7 +443,7 @@
 
     remote(w.at[core], w.at[other], w_send, w_recv, me, partner).wait_send()
     for number, make in enumerate(
-        (up_one, up_two, right_zero, left_zero, right_one, left_one, relay_right, relay_left, far_back)
+        (up_one, up_two, right_zero, left_zero, right_one, left_one, relay_right, below_two, far_back)
     ):
         exists = make(0)[1]
 
@@ -510,6 +506,8 @@
             vmem((TOKENS, FEAT), BF),
             vmem((TOKENS, FEAT), BF),
             vmem((SLOTS, HEAD_DIM, TOKENS), BF),
+            vmem((2, FEAT, FEAT), BF),
+            vmem((2, TOKENS, FEAT), F32),
             vmem((ROWS, HEAD_DIM), BF),
             vmem((TOKENS, FEAT), F32),
             vmem((SLOTS, 1, TOKENS), F32),

time: 42.1 us -> 41.3 us (0.981)
  Pallas kernels: 40.8 us -> 40.3 us
    pallas_call x1, Pallas kernels: 40.1 us -> 39.6 us  [on_device(): pl.pallas_call(kernel, out_shape=(pltpu.VMEM((TOKENS, GROUP * HEAD_DIM),...]
where the time goes in v5:
time: 41.3 us; the launch traced here: 40.9 us
  Pallas kernels  40.3 us (98%)
  between operations  0.64 us (2%)
    pallas_call x1, Pallas kernels, on_device(): pl.pallas_call(kernel, out_shape=(pltpu.VMEM((TOKENS, GROUP * HEAD_DIM),...  39.6 us

profile of v5, /device:TPU:1, one launch (start us, length us, event | category | flops | bytes accessed | tf_op | source)
XLA Modules:
  0.0 40.9 jit_solution(16132336593490557889)
XLA Ops:
  0.6 39.6 %relevance.1 = (bf16[128,512]{1,0:T(8,128)(2,1)S(1)}, f32[1,128]{1,0:T(1,128)S(1)}) custom-call(bf16[128,512]{1,0:T(8,128)(2,1)} %q_hbm.1, bf16[128,128]{1,0:T(8,128)(2,1)} %k_hbm.1, bf16[128,128]{1,0:T(8,128)(2,1)} %v_hbm.1, bf16[512,4096]{1,0:T(8,128)(2,1)} %w_hbm.1, bf16[128,512]{1,0:T(8,128)(2,1)} %rel_hbm.1, s32[64,128]{1,0:T(8,128)} %bitcast.2), custom_call_target="tpu_custom_call" | custom-call | tf_op jit(solution)/shard_map/relevance/pallas_call | solution.py:480
  40.3 0.7 %leave.1 = (bf16[128,512]{1,0:T(8,128)(2,1)}, f32[1,128]{1,0:T(1,128)}) custom-call(bf16[128,512]{1,0:T(8,128)(2,1)S(1)} %get-tuple-element.6.heads, f32[1,128]{1,0:T(1,128)S(1)} %get-tuple-element.7.tokens), custom_call_target="tpu_custom_call" | custom-call | tf_op jit(solution)/shard_map/leave/pallas_call | solution.py:525

commit v6 on v5

--- a/solution.py
+++ b/solution.py
@@ -33,8 +33,8 @@
     q_hbm, k_hbm, v_hbm, w_hbm, rel_hbm, seg_hbm, heads, tokens_ref,
     q, kv, w, rel, seg, score, weight, peak, att, far_out, far_in, right_out, left_out, left_in, right_in, near,
     ratio, cross_out, cross_in, values_flipped, flipped, back, passed, inverse, term_out, term_in,
-    local_sem, w_local_sem, w_send, w_recv, kv_send, kv_recv, a_send, a_recv,
-    rs_send, rs_recv, ag_send, ag_recv, c_send, c_recv, t_send, t_recv,
+    local_sem, w_local_sem, sent, w_recv, kv_send, kv_recv, a_recv,
+    rs_recv, ag_recv, c_recv, t_send, t_recv,
 ):
     me = lax.axis_index("ctx")
     tp = lax.axis_index("tp")
@@ -63,14 +63,14 @@
         pltpu.make_async_copy(k_hbm, kv.at[0, 0], local_sem.at[0]),
         pltpu.make_async_copy(v_hbm, kv.at[0, 1], local_sem.at[1]),
         pltpu.make_async_copy(seg_hbm, seg, local_sem.at[2]),
-        pltpu.make_async_copy(rel_hbm, rel, local_sem.at[3]),
+        pltpu.make_async_copy(rel_hbm, rel, local_sem.at[2]),
     ]
     for h in range(GROUP):
         loads.append(
             pltpu.make_async_copy(
                 q_hbm.at[:, h * HEAD_DIM:(h + 1) * HEAD_DIM],
                 q.at[h * TOKENS:(h + 1) * TOKENS, :],
-                local_sem.at[4],
+                local_sem.at[2],
             )
         )
     for load in loads:
@@ -110,7 +110,7 @@
     def kv_copy(number, half, src, dst, ctx):
         return (
             remote(
-                kv.at[src, half], kv.at[dst, half], kv_send.at[number], kv_recv.at[dst, half], ctx, tp
+                kv.at[src, half], kv.at[dst, half], kv_send, kv_recv.at[dst, half], ctx, tp
             ),
             (ctx >= dst) & (ctx < CTX),
         )
@@ -126,7 +126,7 @@
         @pl.when(me >= slot)
         def _():
             remote(
-                kv.at[slot, half], kv.at[slot, half], kv_send.at[0], kv_recv.at[slot, half], me, tp
+                kv.at[slot, half], kv.at[slot, half], kv_send, kv_recv.at[slot, half], me, tp
             ).wait_recv()
 
     right_src = jnp.where(y < 3, 0, 8)
@@ -192,15 +192,14 @@
         w_copies.append(
             remote(
                 w_hbm.at[:, pl.ds(pl.multiple_of((2 * i + other) * FEAT, FEAT), FEAT)],
-                w.at[core, i], w_send, w_recv, me, partner,
+                w.at[core, i], sent, w_recv, me, partner,
             )
         )
     for copy in w_copies:
         copy.start()
 
-    for load in loads[2:4]:
-        load.wait()
-    pltpu.make_async_copy(q, q, local_sem.at[4]).wait()
+    three = w.at[0, 0, pl.ds(0, 288)]
+    pltpu.make_async_copy(three, three, local_sem.at[2]).wait()
 
     own_seg = jnp.broadcast_to(seg[pl.ds(me, 1), :].astype(F32), (TOKENS, TOKENS)).T
     row_at = lax.broadcasted_iota(jnp.int32, (TOKENS, TOKENS), 0)
@@ -232,19 +231,11 @@
     score_block(4)
 
 
-    @pl.when(y > 0)
+    @pl.when((y == 1) | (y == 2))
     def _():
         for half in range(2):
             arrive(1, half)
-
-            @pl.when(y < 3)
-            def _():
-                start(relay_right(half))
-
-    @pl.when(y == 3)
-    def _():
-        for half in range(2):
-            arrive(3, half)
+            start(relay_right(half))
 
     for half in range(2):
         arrive(8, half)
@@ -259,34 +250,20 @@
 
         start(far_back(half))
 
-    score_block(jnp.where(y > 0, 1, 8))
-
-    one_left = jnp.where(y > 0, 5, 1)
-    one_right = jnp.where(y < 3, 3, 7)
-    for half in range(2):
-        arrive(one_left, half)
-        arrive(one_right, half)
-
-    score_block(jnp.where(y > 0, 8, 1))
-    score_block(5 - jnp.where(y > 0, 0, 2))
-    @pl.when(y == 0)
-    def _():
-        for half in range(2):
-            arrive(5, half)
-
-    @pl.when(y < 3)
-    def _():
-        for half in range(2):
-            arrive(7, half)
-
-    score_block(jnp.where(y > 0, 3, 5))
-    score_block(7)
-    for half in range(2):
-        arrive(2, half)
-    score_block(2)
-    for half in range(2):
-        arrive(6, half)
-    score_block(6)
+    score_block(8)
+    orders = ((3, 7, 2, 6, 1, 5), (1, 5, 3, 7, 2, 6), (1, 2, 5, 6, 3, 7), (1, 3, 2, 6, 7, 5))
+    for i in range(6):
+        by_y = [order[i] for order in orders]
+        slot = jnp.where(y == 0, by_y[0], jnp.where(y == 1, by_y[1], jnp.where(y == 2, by_y[2], by_y[3])))
+        if i == 0:
+            @pl.when((y == 0) | (y == 3))
+            def _():
+                for half in range(2):
+                    arrive(slot, half)
+        else:
+            for half in range(2):
+                arrive(slot, half)
+        score_block(slot)
 
     values = kv[:, 1].reshape(SLOTS * TOKENS, HEAD_DIM)
     for h in range(GROUP):
@@ -305,11 +282,11 @@
         summed = dot_nn(weight[rows, :], values)
         att[core, :, columns] = (summed * inv).astype(BF)
 
-    a_copy = remote(att.at[core], att.at[core], a_send, a_recv, me, partner)
+    a_copy = remote(att.at[core], att.at[core], sent, a_recv, me, partner)
     a_copy.start()
     pltpu.make_async_copy(w.at[core], w.at[core], w_local_sem).wait()
-    remote(w.at[core], w.at[other], w_send, w_recv, me, partner).wait_recv()
-    remote(att.at[other], att.at[other], a_send, a_recv, me, partner).wait_recv()
+    remote(w.at[core], w.at[other], sent, w_recv, me, partner).wait_recv()
+    remote(att.at[other], att.at[other], sent, a_recv, me, partner).wait_recv()
 
     def project(i):
         return dot_nn(att[core], w[core, i]) + dot_nn(att[other], w[other, i])
@@ -317,7 +294,7 @@
     quarter = [pl.ds(i * QUARTER, QUARTER) for i in range(4)]
 
     def rs(kind, i, src, dst, tpi):
-        return remote(src, dst, rs_send, rs_recv.at[4 + i // 2 if kind else i], me, tpi)
+        return remote(src, dst, sent, rs_recv.at[4 + i // 2 if kind else i], me, tpi)
 
     def rs_far(i):
         return rs(0, i, far_out.at[quarter[i]], far_in.at[quarter[i]], x_left if i % 2 else x_right)
@@ -361,7 +338,7 @@
     def ag(kind, i, owner, tpi):
         return remote(
             ratio.at[owner, quarter[i]], ratio.at[owner, quarter[i]],
-            ag_send, ag_recv.at[3 + kind if kind else i], me, tpi,
+            sent, ag_recv.at[3 + kind if kind else i], me, tpi,
         )
 
     def ag_first(i, owner):
@@ -374,7 +351,7 @@
         return ag(2, i, owner, x_left if i % 2 else x_right)
 
     for half in range(2):
-        remote(left_in, left_in, rs_send, rs_recv.at[4 + half], me, x_left).wait_recv()
+        remote(left_in, left_in, sent, rs_recv.at[4 + half], me, x_left).wait_recv()
         for i in (2 * half, 2 * half + 1):
             rows = quarter[i]
             total = near[2, rows, :] + left_in[rows, :].astype(F32) + right_in[rows, :].astype(F32)
@@ -388,14 +365,14 @@
         owner = x_right_i if i % 2 else x_left_i
         ag_first(i, owner).wait_recv()
         ag_relay(i, owner).start()
-    remote(ratio.at[x], ratio.at[x_left_i], ag_send, ag_recv.at[4], me, x_left).wait_recv()
+    remote(ratio.at[x], ratio.at[x_left_i], sent, ag_recv.at[4], me, x_left).wait_recv()
     for owner in (x_left_i, x_right_i):
         back[0] += dot_nt(ratio[owner], w[other, owner])
         back[1] += dot_nt(ratio[owner], w[core, owner])
-    remote(ratio.at[x], ratio.at[x_far_i], ag_send, ag_recv.at[5], me, x_left).wait_recv()
+    remote(ratio.at[x], ratio.at[x_far_i], sent, ag_recv.at[5], me, x_left).wait_recv()
     back_other = back[0] + dot_nn(ratio[x_far_i], flipped[other])
     cross_out[...] = back_other.astype(BF)
-    cross = remote(cross_out, cross_in, c_send, c_recv, me, partner)
+    cross = remote(cross_out, cross_in, sent, c_recv, me, partner)
     cross.start()
     back_own = back[1] + dot_nn(ratio[x_far_i], flipped[core])
     cross.wait_recv()
@@ -419,13 +396,15 @@
             me - slot, tp,
         )
 
-    for slot in range(SLOTS - 1, 0, -1):
-        term_out[slot] = term(slot)
-    for slot in range(SLOTS - 1, 0, -1):
-        @pl.when(me >= slot)
-        def _():
-            term_copy(slot).start()
-
+    for batch in ((8, 7, 6, 5), (4, 3, 2, 1)):
+        for slot in batch:
+            term_out[slot] = term(slot)
+        for slot in batch:
+            @pl.when(me >= slot)
+            def _():
+                term_copy(slot).start()
+
+    for slot in range(1, SLOTS):
         @pl.when(me + slot >= CTX)
         def _():
             term_in[slot] = jnp.zeros((1, TOKENS), F32)
@@ -441,21 +420,19 @@
         own = own + term_in[slot]
     tokens_ref[...] = own
 
-    remote(w.at[core], w.at[other], w_send, w_recv, me, partner).wait_send()
-    for number, make in enumerate(
-        (up_one, up_two, right_zero, left_zero, right_one, left_one, relay_right, below_two, far_back)
+    copies = 0
+    for make in (
+        up_one, up_two, right_zero, left_zero, right_one, left_one, relay_right, below_two, far_back
     ):
-        exists = make(0)[1]
-
-        @pl.when(exists)
-        def _():
-            remote(kv.at[0], kv.at[0], kv_send.at[number], kv_recv.at[0, 0], me, tp).wait_send()
-
-    a_copy.wait_send()
-    twelve = w.at[0, 0, pl.ds(0, 3 * TOKENS)]
-    remote(twelve, twelve, rs_send, rs_recv.at[0], me, x_left).wait_send()
-    remote(twelve, twelve, ag_send, ag_recv.at[0], me, x_left).wait_send()
-    cross.wait_send()
+        copies = copies + jnp.where(make(0)[1], 1, 0)
+    for count in range(1, SLOTS + 1):
+        @pl.when(copies == count)
+        def _():
+            some = kv.at[pl.ds(0, count)]
+            remote(some, some, kv_send, kv_recv.at[0, 0], me, tp).wait_send()
+
+    everything = w.at[:, 0:3]
+    remote(everything, everything, sent, w_recv, me, partner).wait_send()
     for count in range(1, SLOTS):
         @pl.when(jnp.minimum(SLOTS - 1, me) == count)
         def _():
@@ -512,10 +489,8 @@
             vmem((TOKENS, FEAT), F32),
             vmem((SLOTS, 1, TOKENS), F32),
             vmem((SLOTS, 1, TOKENS), F32),
-            dma((5,)), dma, dma, dma,
-            dma((9,)), dma((SLOTS, 2)), dma, dma,
-            dma, dma((6,)), dma, dma((6,)), dma, dma,
-            dma, dma,
+            dma((3,)), dma, dma, dma, dma, dma((SLOTS, 2)), dma,
+            dma((6,)), dma((6,)), dma, dma, dma,
         ],
         compiler_params=pltpu.CompilerParams(
             collective_id=0, has_side_effects=True, vmem_limit_bytes=60 << 20

time: 41.3 us -> 41 us (level)
  Pallas kernels: 40.3 us -> 39.6 us
    pallas_call x1, Pallas kernels: 39.6 us -> 39 us  [on_device(): pl.pallas_call(kernel, out_shape=(pltpu.VMEM((TOKENS, GROUP * HEAD_DIM),...]
where the time goes in v6:
time: 41 us; the launch traced here: 40.3 us
  Pallas kernels  39.6 us (97%)
  between operations  0.64 us (2%)
    pallas_call x1, Pallas kernels, on_device(): pl.pallas_call(kernel, out_shape=(pltpu.VMEM((TOKENS, GROUP * HEAD_DIM),...  39 us

profile of v6, /device:TPU:1, one launch (start us, length us, event | category | flops | bytes accessed | tf_op | source)
XLA Modules:
  0.0 40.3 jit_solution(4940085278119042069)
XLA Ops:
  0.6 39.0 %relevance.1 = (bf16[128,512]{1,0:T(8,128)(2,1)S(1)}, f32[1,128]{1,0:T(1,128)S(1)}) custom-call(bf16[128,512]{1,0:T(8,128)(2,1)} %q_hbm.1, bf16[128,128]{1,0:T(8,128)(2,1)} %k_hbm.1, bf16[128,128]{1,0:T(8,128)(2,1)} %v_hbm.1, bf16[512,4096]{1,0:T(8,128)(2,1)} %w_hbm.1, bf16[128,512]{1,0:T(8,128)(2,1)} %rel_hbm.1, s32[64,128]{1,0:T(8,128)} %bitcast.2), custom_call_target="tpu_custom_call" | custom-call | tf_op jit(solution)/shard_map/relevance/pallas_call | solution.py:457
  39.6 0.7 %leave.1 = (bf16[128,512]{1,0:T(8,128)(2,1)}, f32[1,128]{1,0:T(1,128)}) custom-call(bf16[128,512]{1,0:T(8,128)(2,1)S(1)} %get-tuple-element.6.heads, f32[1,128]{1,0:T(1,128)S(1)} %get-tuple-element.7.tokens), custom_call_target="tpu_custom_call" | custom-call | tf_op jit(solution)/shard_map/leave/pallas_call | solution.py:500

commit v7 on v6

--- a/solution.py
+++ b/solution.py
@@ -88,10 +88,6 @@
     greet(y_right, tp)
     greet(y_left, tp)
 
-    @pl.when(me < CTX - 4)
-    def _():
-        greet(me + 4, tp)
-
     @pl.when(me >= 4)
     def _():
         greet(me - 4, tp)
@@ -104,7 +100,7 @@
                 kv[d] = jnp.zeros((2, TOKENS, HEAD_DIM), BF)
 
     pl.semaphore_wait(
-        barrier, 6 + jnp.where(me < CTX - 4, 1, 0) + jnp.where(me >= 4, 1, 0)
+        barrier, 6 + jnp.where(me < CTX - 4, 1, 0)
     )
 
     def kv_copy(number, half, src, dst, ctx):

time: 41 us -> 41 us (level)
  no operation moved by 1% of the time
where the time goes in v7:
time: 41 us; the launch traced here: 40.3 us
  Pallas kernels  39.6 us (97%)
  between operations  0.64 us (2%)
    pallas_call x1, Pallas kernels, on_device(): pl.pallas_call(kernel, out_shape=(pltpu.VMEM((TOKENS, GROUP * HEAD_DIM),...  39 us

profile of v7, /device:TPU:1, one launch (start us, length us, event | category | flops | bytes accessed | tf_op | source)
XLA Modules:
  0.0 40.3 jit_solution(1452919571219997265)
XLA Ops:
  0.6 39.0 %relevance.1 = (bf16[128,512]{1,0:T(8,128)(2,1)S(1)}, f32[1,128]{1,0:T(1,128)S(1)}) custom-call(bf16[128,512]{1,0:T(8,128)(2,1)} %q_hbm.1, bf16[128,128]{1,0:T(8,128)(2,1)} %k_hbm.1, bf16[128,128]{1,0:T(8,128)(2,1)} %v_hbm.1, bf16[512,4096]{1,0:T(8,128)(2,1)} %w_hbm.1, bf16[128,512]{1,0:T(8,128)(2,1)} %rel_hbm.1, s32[64,128]{1,0:T(8,128)} %bitcast.2), custom_call_target="tpu_custom_call" | custom-call | tf_op jit(solution)/shard_map/relevance/pallas_call | solution.py:453
  39.6 0.7 %leave.1 = (bf16[128,512]{1,0:T(8,128)(2,1)}, f32[1,128]{1,0:T(1,128)}) custom-call(bf16[128,512]{1,0:T(8,128)(2,1)S(1)} %get-tuple-element.6.heads, f32[1,128]{1,0:T(1,128)S(1)} %get-tuple-element.7.tokens), custom_call_target="tpu_custom_call" | custom-call | tf_op jit(solution)/shard_map/leave/pallas_call | solution.py:496
